TPU v7x, 512 devices: a whole 4x8x8 slice. The times are simulated.
512 devices in a mesh: seq: 8 (over y_lo, x), fsdp: 64 (over z, y_hi, core).
Axes of the slice: x: 4, y: 8 (y_hi: 4, y_lo: 2; y = y_hi * 2 + y_lo), z: 8, core: 2. Of those that a mesh axis runs over, the one named last changes fastest.
Arguments:
- hidden: bfloat16 [2048, 8192], P('seq', 'fsdp'), may hold values from -28 to 28
- q_weight: bfloat16 [8192, 8192], P('fsdp'), may hold values from -0.0625 to 0.0625
- kv_weight: bfloat16 [2048, 8192], P(None, 'fsdp'), may hold values from -0.0625 to 0.0625
- d_attended: bfloat16 [2048, 8192], P('seq', 'fsdp'), may hold values from -6 to 6
- doc_lengths: int32 [4], replicated, may hold values from 1 to 1536, as said below
- prompt_pos: int32 [128], replicated, may hold values from 0 to 2047, as said below
Outputs:
- attended: bfloat16 [2048, 8192], P('seq', 'fsdp')
- prompt_grad: float32 [128, 8192], P('seq', 'fsdp')
Inputs may be any that keep to these rules, and one draw needn't show every extreme that they name: `doc_lengths`: 4 document lengths in pack order that sum to 2048; exactly one is 1536, at a position that varies from draw to draw, and the others are at least 1. `prompt_pos`: for every block i of 256 rows, entries i * 16 to (i + 1) * 16 - 1 are distinct rows of that block in rising order; row 0 and row 2047 are always among them.
All inputs are finite; a program needn't handle non-finite values.
Results may differ from a plain program's by a relative error of at most 0.017.
The roundings to bfloat16 on the way count: a program that leaves them out, or rounds other values in their place, can miss the bound.
Values may be sent and summed in bfloat16 or wider, within the bound.
A program may use at most 64 MiB of HBM per device.

v0:
```python
import math

import jax
import jax.numpy as jnp
from jax import lax
from jax.sharding import PartitionSpec as P

GROUP = 8


rope_theta = 1000000.0


def locate(tokens, doc_lengths):
    doc_ends = jnp.cumsum(doc_lengths)
    segment = jnp.sum((tokens[:, None] >= doc_ends[None, :]).astype(jnp.int32), axis=1)
    doc_starts = doc_ends - doc_lengths
    picked = segment[:, None] == jnp.arange(doc_lengths.shape[0], dtype=jnp.int32)[None, :]
    opening = jnp.sum(jnp.where(picked, doc_starts[None, :], 0), axis=1)
    return (segment, tokens - opening)


def rotate(vectors, positions, factor):
    halfway = vectors.shape[-1] // 2
    steps_up = jnp.arange(halfway, dtype=jnp.float32)
    frequency = jnp.exp(steps_up * (-2.0 * math.log(rope_theta) / vectors.shape[-1]))
    angles = positions.astype(jnp.float32)[:, None] * frequency[None, :]
    cosine = jnp.cos(angles)
    sine_part = jnp.sin(angles)
    leading = vectors[..., :halfway]
    trailing = vectors[..., halfway:]
    return jnp.concatenate(
        [
            leading * cosine - factor * trailing * sine_part,
            trailing * cosine + factor * leading * sine_part,
        ],
        axis=-1,
    )


def per_device(hidden, q_weight, kv_weight, d_attended, doc_lengths, prompt_pos):
    seq_count = lax.axis_size("seq")
    row_count = hidden.shape[0]
    head_dim = q_weight.shape[0]
    kv_width = kv_weight.shape[0]
    seq_length = row_count * seq_count
    prompt_count = prompt_pos.shape[0]
    prompt_local = prompt_count // seq_count
    seq_rank = lax.axis_index("seq")
    fsdp_rank = lax.axis_index("fsdp")
    group_index = fsdp_rank // GROUP
    score_scale = 1.0 / math.sqrt(head_dim)
    first_row = seq_rank * row_count
    all_tokens = jnp.arange(seq_length, dtype=jnp.int32)
    segment_all, place_all = locate(all_tokens, doc_lengths)
    own_tokens = first_row + jnp.arange(row_count, dtype=jnp.int32)
    segment_own = lax.dynamic_slice_in_dim(segment_all, first_row, row_count)
    place_own = lax.dynamic_slice_in_dim(place_all, first_row, row_count)
    kv_partial = lax.dot_general(
        hidden, kv_weight, (((1,), (1,)), ((), ())), preferred_element_type=jnp.float32
    )
    kv_summed = lax.psum(kv_partial, "fsdp")
    kv_group = lax.dynamic_slice_in_dim(
        kv_summed, group_index * 2 * head_dim, 2 * head_dim, 1
    ).astype(jnp.bfloat16)
    key_own = rotate(kv_group[:, :head_dim].astype(jnp.float32), place_own, 1.0).astype(
        jnp.bfloat16
    )
    kv_block = jnp.concatenate([key_own, kv_group[:, head_dim:]], axis=1)
    kv_full = lax.all_gather(kv_block, "seq", axis=0, tiled=True)
    q_pre = lax.dot_general(
        lax.all_gather(hidden, "fsdp", axis=1, tiled=True),
        q_weight,
        (((1,), (1,)), ((), ())),
        preferred_element_type=jnp.float32,
    )
    own_query = rotate(q_pre, place_own, 1.0).astype(jnp.bfloat16)
    block_len = 512
    block_count = seq_length // block_len
    key_blocks = kv_full[:, :head_dim].reshape(block_count, block_len, head_dim)
    value_blocks = kv_full[:, head_dim:].reshape(block_count, block_len, head_dim)
    key_segments = segment_all.reshape(block_count, block_len)
    key_tokens = all_tokens.reshape(block_count, block_len)
    raw_scores = (
        jnp.einsum("tc,bkc->btk", own_query, key_blocks, preferred_element_type=jnp.float32)
        * score_scale
    )
    allowed = (key_segments[:, None, :] == segment_own[None, :, None]) & (
        key_tokens[:, None, :] <= own_tokens[None, :, None]
    )
    scores = jnp.where(allowed, raw_scores, -jnp.inf)
    row_max = jnp.max(scores, axis=(0, 2))
    exponent_terms = jnp.exp(scores - row_max[None, :, None])
    row_sum = jnp.sum(exponent_terms, axis=(0, 2))
    attention_probs = (exponent_terms / row_sum[None, :, None]).astype(jnp.bfloat16)
    attended_sum = jnp.einsum(
        "btk,bkc->tc", attention_probs, value_blocks, preferred_element_type=jnp.float32
    )
    attended = attended_sum.astype(jnp.bfloat16)
    rowdot = jnp.sum(d_attended.astype(jnp.float32) * attended.astype(jnp.float32), axis=1)
    local_prompts = (
        lax.dynamic_slice_in_dim(prompt_pos, seq_rank * prompt_local, prompt_local) - first_row
    )
    row_probs = jnp.take(attention_probs, local_prompts, axis=1)
    row_upstream = jnp.take(d_attended, local_prompts, axis=0)
    row_dprobs = jnp.einsum(
        "pc,bkc->bpk", row_upstream, value_blocks, preferred_element_type=jnp.float32
    )
    row_dot = jnp.take(rowdot, local_prompts)
    row_dscores = (row_probs.astype(jnp.float32) * (row_dprobs - row_dot[None, :, None])).astype(
        jnp.bfloat16
    )
    query_grad = (
        jnp.einsum("bpk,bkc->pc", row_dscores, key_blocks, preferred_element_type=jnp.float32)
        * score_scale
    )
    query_grad = rotate(query_grad, jnp.take(place_own, local_prompts), -1.0).astype(jnp.bfloat16)
    block_of = prompt_pos // block_len
    column_of = prompt_pos % block_len
    col_probs = attention_probs[block_of, :, column_of]
    col_values = value_blocks[block_of, column_of]
    col_dprobs = lax.dot_general(
        col_values, d_attended, (((1,), (1,)), ((), ())), preferred_element_type=jnp.float32
    )
    col_dscores = (col_probs.astype(jnp.float32) * (col_dprobs - rowdot[None, :])).astype(
        jnp.bfloat16
    )
    key_grad = jnp.dot(col_dscores, own_query, preferred_element_type=jnp.float32) * score_scale
    key_grad = rotate(key_grad, jnp.take(place_all, prompt_pos), -1.0)
    value_grad = jnp.dot(col_probs, d_attended, preferred_element_type=jnp.float32)
    kv_grad_mine = jnp.concatenate([key_grad, value_grad], axis=1)
    seq_summed = lax.psum_scatter(kv_grad_mine, "seq", scatter_dimension=0, tiled=True)
    wide_own = jnp.zeros((prompt_local, kv_width), jnp.float32)
    wide_own = lax.dynamic_update_slice_in_dim(wide_own, seq_summed, group_index * 2 * head_dim, 1)
    kv_grad = lax.psum(wide_own, "fsdp").astype(jnp.bfloat16)
    q_part = lax.psum_scatter(
        lax.dot_general(
            q_weight, query_grad, (((0,), (1,)), ((), ())), preferred_element_type=jnp.float32
        ),
        "fsdp",
        scatter_dimension=0,
        tiled=True,
    )
    kv_part = jnp.dot(kv_grad, kv_weight, preferred_element_type=jnp.float32)
    prompt_grad = q_part.T + kv_part
    return (attended, prompt_grad)


def solution(mesh):
    placed = (P("seq", "fsdp"), P("fsdp", None), P(None, "fsdp"), P("seq", "fsdp"), P(), P())
    return jax.shard_map(
        per_device,
        mesh=mesh,
        in_specs=placed,
        out_specs=(P("seq", "fsdp"), P("seq", "fsdp")),
        check_vma=False,
    )
```

profile of v0, /device:TPU:1, one launch (start us, length us, event | category | flops | bytes accessed | tf_op | source)
XLA Modules:
  0.0 724.0 jit_solution(16325572370149899096)
XLA Ops:
  7.2 0.0 copy-start
  7.2 0.0 copy-start.6
  7.2 0.0 all-gather.5.cloned.1.call-start
  7.2 0.7 all-gather.5.cloned.1.call-update
  7.9 0.0 all-gather.3.cloned.1.call-start
  8.0 2.8 fusion.74
  10.8 0.0 copy-done.6
  10.8 0.2 reduce-window.8
  11.0 0.1 convert_reduce_fusion
  11.1 0.1 select_reduce_fusion
  11.2 0.1 fusion.71
  11.3 307.9 %all-reduce.2 = bf16[256,2048]{0,1:T(8,128)(2,1)S(1)} all-reduce(f32[256,2048]{0,1:T(8,128)} %fusion.74), channel_id=1, replica_groups=mesh['seq'=8,'fsdp'=64] {'fsdp'}, use_global_device_ids=true, to_apply=%region_2.3 | all-reduce | flops 524288 | bytes 3145728 | tf_op jit(solution)/shard_map/psum | solution.py:62
  319.3 0.0 copy-start.2
  319.3 0.0 copy-start.4
  319.3 0.0 all-gather.5.cloned.1.call-done
  319.3 0.0 copy-done
  319.3 3.7 fusion.75
  323.1 0.3 fusion.27
  323.4 0.7 pad_maximum_fusion
  324.1 0.0 all-gather.3.cloned.1.call-update
  324.1 0.0 reduce-scatter.7.cloned.1.call-start
  324.1 0.1 dynamic_slice.12
  324.2 0.0 copy-done.2
  324.2 0.1 copy.51
  324.4 0.6 compare_and_fusion
  325.0 0.6 gather_fusion.1
  325.6 0.7 gather_fusion.3
  326.2 1.1 gather_fusion.6
  327.4 0.5 select_convert_fusion
  328.0 0.5 fusion.65
  328.5 39.3 %all-gather.3.cloned.1.call-done = bf16[2048,256]{0,1:T(8,128)(2,1)} async-done(((bf16[256,256]{0,1:T(8,128)(2,1)}), bf16[2048,256]{0,1:T(8,128)(2,1)}) %all-gather.3.cloned.1.call-update) | async-done | bytes 1048592 | tf_op jit(solution)/shard_map/all_gather | solution.py:70
  367.8 2.1 fusion.72
  369.9 0.3 copy.61
  370.1 0.0 copy-done.3
  370.2 0.0 copy-start.1
  370.2 0.7 fusion.73
  370.8 0.1 copy-done.1
  371.0 0.4 fusion
  371.3 0.3 divide_convert_fusion
  371.7 1.8 copy.48
  373.5 1.8 gather_fusion
  375.3 2.0 copy.62
  377.4 1.1 gather_fusion.4
  378.5 2.5 gather_fusion.5
  381.0 1.4 multiply_reduce_fusion
  382.5 0.0 copy-start.5
  382.5 0.7 gather_fusion.2
  383.1 0.6 broadcast_select_fusion
  383.8 0.2 fusion.76
  384.0 1.1 convolution_multiply_fusion
  385.1 0.9 fusion.38
  385.9 0.8 copy.59
  386.7 0.0 reduce-scatter.7.cloned.1.call-update
  386.7 0.0 reduce-scatter.5.cloned.1.call-start
  386.8 1.6 fusion.9
  388.4 0.1 fusion.46
  388.5 1.2 convolution_bitcast_fusion
  389.8 0.0 reduce-scatter.5.cloned.1.call-update
  389.8 0.7 copy.54
  390.5 39.5 %reduce-scatter.7.cloned.1.call-done = f32[16,256]{1,0:T(8,128)} async-done(((f32[128,256]{1,0:T(8,128)}), f32[16,256]{1,0:T(8,128)}) %reduce-scatter.7.cloned.1.call-update) | async-done | bytes 16400
  430.0 0.8 copy.60
  430.9 0.1 broadcast_in_dim.88
  431.0 284.4 %all-reduce.3 = bf16[16,2048]{0,1:T(8,128)(2,1)} all-reduce(f32[16,2048]{0,1:T(8,128)S(1)} %constant_dynamic-update-slice_fusion), channel_id=1, replica_groups=mesh['seq'=8,'fsdp'=64] {'fsdp'}, use_global_device_ids=true, to_apply=%region_9.10 | all-reduce | flops 32768 | bytes 196608 | tf_op jit(solution)/shard_map/psum | solution.py:135
  715.4 2.1 convolution_add_fusion
  (17 shorter events, 0.1 us)
Async XLA Ops:
  7.2 312.2 %copy-start = (bf16[128,8192]{1,0:T(8,128)(2,1)S(1)}, bf16[128,8192]{1,0:T(8,128)(2,1)}, u32[]{:S(2)}) copy-start(bf16[128,8192]{1,0:T(8,128)(2,1)} %param.7) | copy-start | bytes 6291460
  7.2 3.7 copy-start.6
  7.2 312.1 %all-gather.5.cloned.1.call-start = ((), (), s32[]{:S(2)}) async-start(), calls=%async_computation.3 | async-start | bytes 4259840 | tf_op jit(solution)/shard_map/all_gather | solution.py:72
  7.9 359.8 %all-gather.3.cloned.1.call-start = ((), (), s32[]{:S(2)}) async-start(), calls=%async_computation.2 | async-start | bytes 1179648 | tf_op jit(solution)/shard_map/all_gather | solution.py:70
  319.3 5.0 copy-start.2
  319.3 5.1 copy-start.4
  324.1 105.9 %reduce-scatter.7.cloned.1.call-start = ((), (), s32[]{:S(2)}) async-start(), calls=%async_computation.5 | async-start | bytes 147456
  325.0 45.2 %copy-start.3 = (s32[16]{0:T(128)}, s32[16]{0:T(128)S(1)}, u32[]{:S(2)}) copy-start(s32[16]{0:T(128)S(1)} %get-tuple-element.13) | copy-start | bytes 196
  370.2 0.8 copy-start.1
  382.5 5.9 copy-start.5
  386.7 328.7 %reduce-scatter.5.cloned.1.call-start = ((), (), s32[]{:S(2)}) async-start(), calls=%async_computation.4 | async-start | bytes 532480 | tf_op jit(solution)/shard_map/reduce_scatter | solution.py:136
Sparse Core Ops, SparseCore 0:
  11.2 95.0 all-gather.4
  324.2 43.4 all-gather.2
  386.8 43.1 reduce-scatter.6
  434.4 139.5 reduce-scatter.4
where the time goes:
time: 730 us; the launch traced here: 724 us
  blocking collectives  592 us (81%)
  waiting for transfers between devices  79.6 us (11%)
  local copies, waits for them, and re-layouts  17.6 us (2%)
  matrix products  14.9 us (2%)
  between operations  14 us (2%)
    psum x1, blocking collectives, per_device(): kv_summed = lax.psum(kv_partial, 'fsdp')  308 us
    psum x1, blocking collectives, per_device(): kv_grad = lax.psum(wide_own, 'fsdp').astype(jnp.bfloat16)  284 us
    unnamed x5, waiting for transfers between devices  40.2 us
    all_gather x1, waiting for transfers between devices, per_device(): kv_full = lax.all_gather(kv_block, 'seq', axis=0, tiled=True)  39.3 us
  transfers between devices with their start and end apart: 4, of which 2 were waited for; matrix products, arithmetic and copies ran while one was open for 2% of the time, Pallas kernels for 0%

commit v1 on v0

v1 whole, which is shorter than its diff:
```python
import functools
import math

import jax
import jax.numpy as jnp
from jax import lax
from jax.experimental import pallas as pl
from jax.experimental.pallas import tpu as pltpu
from jax.sharding import PartitionSpec as P

ROPE_THETA = 1000000.0
MESH = pl.DeviceIdType.MESH
F32 = jnp.float32
BF16 = jnp.bfloat16
VMEM = pltpu.VMEM
DMA = pltpu.SemaphoreType.DMA

X, YL, YH, Z, C = 4, 2, 4, 8, 2
ROWS, HD, FB = 256, 128, 128


def nt(a, b):
    return lax.dot_general(a, b, (((1,), (1,)), ((), ())), preferred_element_type=F32)


class Place:
    def __init__(self):
        self.s = lax.axis_index("seq")
        self.f = lax.axis_index("fsdp")
        self.x = self.s % X
        self.yl = self.s // X
        self.z = self.f // (YH * C)
        self.yh = (self.f // C) % YH
        self.c = self.f % C
        self.o = 1 - self.c

    def fid(self, z, yh, c):
        return (z * YH + yh) * C + c


class Wires:
    def __init__(self):
        self.open = []

    def make(self, src, dst, ss, rs, seq, fs):
        return pltpu.make_async_remote_copy(
            src_ref=src, dst_ref=dst, send_sem=ss, recv_sem=rs,
            device_id={"seq": seq, "fsdp": fs}, device_id_type=MESH)

    def send(self, *args):
        copy = self.make(*args)
        copy.start()
        self.open.append(copy)

    def finish(self):
        for copy in self.open:
            copy.wait_send()


def nn(a, b):
    return lax.dot_general(a, b, (((1,), (0,)), ((), ())), preferred_element_type=F32)


def tn(a, b):
    return lax.dot_general(a, b, (((0,), (0,)), ((), ())), preferred_element_type=F32)


def lanes(k, n=128):
    return pl.ds(pl.multiple_of(k * n, n), n)


STEP = -2.0 * math.log(ROPE_THETA) / HD
SCALE = 1.0 / math.sqrt(HD)
SEQ, NP, PL = 2048, 128, 16


def openings(tokens, doc):
    end = jnp.int32(0)
    start = jnp.zeros_like(tokens)
    for i in range(4):
        end = end + doc[i]
        start = start + jnp.where(tokens >= end, doc[i], 0)
    return start


def whole(hid, qw, kvw, kvflat, dat, doc, prow, att_out, pg_out,
          H, W2, KW, PS, PR, SS, SR, KB, QP, QR, KVT, COS, SIN, QB, PB, CM, KVL,
          QG, GP, GR, G1, GX, G2, GY, DK, DKV, QF, QY, QS, QZ,
          s_h, r_h, r_h2, s_hz, s_w, r_w, l_w, s_k, r_k, l_k, s_p, r_p, s_s, r_s,
          s_b, r_b, s_x, r_x, s_c, r_c, s_q, r_q, l_v,
          s_g, r_g, s_d1, r_d1, s_d2, r_d2, s_d3, r_d3, s_d4, r_d4, s_e2, r_e2, s_e3, r_e3):
    d = Place()
    s, f, x, yl, z, yh, c, o = d.s, d.f, d.x, d.yl, d.z, d.yh, d.c, d.o
    mate = d.fid(z, yh, o)
    zup, zdn = (z + 1) % Z, (z + Z - 1) % Z
    w = Wires()

    bar = pltpu.get_barrier_semaphore()
    peers = [(s, mate)]
    ypeers = []
    for e in range(1, YH * YL):
        y = (yh * YL + yl + e) % (YH * YL)
        ypeers.append((y // YL, y % YL))
        peers.append(((y % YL) * X + x, d.fid(z, y // YL, c)))
    xpeers = [(x + e) % X for e in range(1, X)]
    for xx in xpeers:
        peers.append((yl * X + xx, f))
    zpeers = [(z + e) % Z for e in range(1, Z)]
    for zz in zpeers:
        peers.append((s, d.fid(zz, yh, c)))
        peers.append((s, d.fid(zz, yh, o)))
    for ps, pf in peers:
        pl.semaphore_signal(bar, inc=1, device_id={"seq": ps, "fsdp": pf}, device_id_type=MESH)
    pl.semaphore_wait(bar, len(peers))

    def hblock(zz, yy):
        return H.at[:, lanes(zz * YH + yy)]

    def wslice(yy):
        return kvw.at[:, yy // 2, :, yy % 2]

    def recv(ref, sem):
        w.make(ref, ref, s_q, sem, s, mate).wait_recv()

    for e in range(1, YH):
        yy = (yh + e) % YH
        w.send(hid, hblock(z, yh), s_h.at[e - 1], r_h.at[z * YH + yh], s, d.fid(z, yy, c))
    for i, zz in enumerate((zup, zdn)):
        w.send(hid, hblock(z, yh), s_hz.at[i, 0, 0], r_h.at[z * YH + yh], s, d.fid(zz, yh, c))
    for e in range(1, YH):
        yy = (yh + e) % YH
        w.send(wslice(yy), KW.at[:, :, :, lanes(yh)], s_k.at[e - 1], r_k.at[yh], s, d.fid(z, yy, c))
    kown = pltpu.make_async_copy(wslice(yh), KW.at[:, :, :, lanes(yh)], l_k)
    kown.start()

    def wload(k, _):
        pltpu.make_async_copy(qw.at[:, pl.ds(pl.multiple_of(k * 256 + c * 128, 128), 128)],
                              W2.at[pl.ds(c * 128, 128), lanes(k)], l_w).start()
        w.make(qw.at[:, pl.ds(pl.multiple_of(k * 256 + o * 128, 128), 128)],
               W2.at[pl.ds(c * 128, 128), lanes(k)], s_w, r_w, s, mate).start()
        return 0
    lax.fori_loop(0, Z * YH, wload, 0)
    kvload = pltpu.make_async_copy(kvflat, KVL, l_v)
    kvload.start()
    H[:, lanes(z * YH + yh)] = hid[...]

    tok = s * ROWS + lax.broadcasted_iota(jnp.int32, (1, ROWS), 1)
    place = (tok - openings(tok, doc)).astype(F32)
    freq = jnp.exp(lax.broadcasted_iota(jnp.int32, (HD // 2, 1), 0).astype(F32) * STEP)
    angle = freq * place
    COS[...] = jnp.cos(angle)
    SIN[...] = jnp.sin(angle)
    prompts = prow[...]
    for i in range(8):
        at = i * 256 + lax.broadcasted_iota(jnp.int32, (256, NP), 0)
        CM[pl.ds(i * 256, 256), :] = jnp.where(at == prompts, 1.0, 0.0).astype(BF16)
    near = lax.broadcasted_iota(jnp.int32, (PL, NP), 1) == (
        s * PL + lax.broadcasted_iota(jnp.int32, (PL, NP), 0))
    own_p = jnp.sum(jnp.where(near, prompts.astype(F32), 0.0), axis=1, keepdims=True).astype(jnp.int32)
    pick = jnp.where(lax.broadcasted_iota(jnp.int32, (PL, ROWS), 1) == own_p - s * ROWS,
                     1.0, 0.0).astype(BF16)
    lane = lax.broadcasted_iota(jnp.int32, (1, HD), 1)
    freq_l = jnp.exp(jnp.where(lane < 64, lane, lane - 64).astype(F32) * STEP)
    angle_p = (own_p - openings(own_p, doc)).astype(F32) * freq_l
    cos_p = jnp.cos(angle_p)
    sin_p = jnp.where(lane < 64, 1.0, -1.0) * jnp.sin(angle_p)

    def back(u):
        return u * cos_p + pltpu.roll(u, 64, 1) * sin_p

    half = ROWS // 2

    def forward(step):
        up, dn = (z + Z - step) % Z, (z + step) % Z
        for e in range(YH):
            yy = (yh + e) % YH
            if step == 0:
                if e == 0:
                    continue
                recv(hblock(z, yy), r_h.at[z * YH + yy])
                w.send(hblock(z, yy), hblock(z, yy), s_hz.at[0, step, e], r_h.at[z * YH + yy], s, d.fid(zup, yh, c))
                w.send(hblock(z, yy), hblock(z, yy), s_hz.at[1, step, e], r_h.at[z * YH + yy], s, d.fid(zdn, yh, c))
            elif step < 3:
                recv(hblock(up, yy), r_h.at[up * YH + yy])
                w.send(hblock(up, yy), hblock(up, yy), s_hz.at[0, step, e], r_h.at[up * YH + yy], s, d.fid(zup, yh, c))
                recv(hblock(dn, yy), r_h.at[dn * YH + yy])
                w.send(hblock(dn, yy), hblock(dn, yy), s_hz.at[1, step, e], r_h.at[dn * YH + yy], s, d.fid(zdn, yh, c))
            else:
                top = H.at[pl.ds(0, half), lanes(up * YH + yy)]
                recv(hblock(up, yy), r_h.at[up * YH + yy])
                w.send(top, top, s_hz.at[0, step, e], r_h.at[up * YH + yy], s, d.fid(zup, yh, c))
                bot = H.at[pl.ds(half, half), lanes(dn * YH + yy)]
                recv(hblock(dn, yy), r_h.at[dn * YH + yy])
                w.send(bot, bot, s_hz.at[1, step, e], r_h2.at[yy], s, d.fid(zdn, yh, c))

    def gain(zz):
        cols = pl.ds(pl.multiple_of(zz * 512, 512), 512)
        part = nt(W2[:, cols], H[:, cols])
        QP[0] = QP[0] + part[:128]
        QP[1] = QP[1] + part[128:]

    forward(0)
    mine_w, other_w = W2.at[pl.ds(c * 128, 128)], W2.at[pl.ds(o * 128, 128)]
    pltpu.make_async_copy(mine_w, mine_w, l_w).wait()
    recv(other_w, r_w)
    w.make(other_w, other_w, s_w, r_w, s, mate).wait_send()
    QP[...] = jnp.zeros_like(QP)
    gain(z)
    forward(1)
    gain((z + 1) % Z)
    gain((z + Z - 1) % Z)
    forward(2)
    gain((z + 2) % Z)
    gain((z + Z - 2) % Z)
    kown.wait()
    for e in range(1, YH):
        yy = (yh + e) % YH
        recv(KW.at[:, :, :, lanes(yy)], r_k.at[yy])
    mine = pl.ds(pl.multiple_of(z * 512, 512), 512)
    for g in range(Z):
        part = nt(KW[g].reshape(64, 512), H[:, mine]).reshape(2, 2, 16, ROWS)
        PS[0, g] = part[:, 0]
        PS[1, g] = part[:, 1]
    w.send(PS.at[o], PR, s_p, r_p, s, mate)
    forward(3)
    recv(PR, r_p)
    SS[...] = PS[c] + PR[...]
    for e, zz in enumerate(zpeers):
        w.send(SS.at[zz], SR.at[z], s_s.at[e], r_s.at[z], s, d.fid(zz, yh, c))
    SR[z] = SS[z]
    gain((z + 3) % Z)
    gain((z + Z - 3) % Z)
    for zz in zpeers:
        recv(SR.at[zz], r_s.at[zz])
    total = SR[0]
    for i in range(1, Z):
        total = total + SR[i]
    kvb = total.astype(BF16)
    kf = kvb.astype(F32)
    b16 = pl.ds(pl.multiple_of((yh % 2) * 32 + c * 16, 16), 16)
    ck, sk = COS[b16, :], SIN[b16, :]
    iskey = yh < 2
    KB[0] = jnp.where(iskey, kf[0] * ck - kf[1] * sk, kf[0]).astype(BF16)
    KB[1] = jnp.where(iskey, kf[1] * ck + kf[0] * sk, kf[1]).astype(BF16)

    def kblock(yy, ll, xx):
        return KVT.at[yy // 2, :, yy % 2, c, :, lanes(ll * X + xx, ROWS)]

    for e, (yy, ll) in enumerate(ypeers):
        w.send(KB, kblock(yh, yl, x), s_b.at[e], r_b.at[yh, yl], ll * X + x, d.fid(z, yy, c))
    KVT[yh // 2, :, yh % 2, c, :, lanes(s, ROWS)] = KB[...]
    for i, xx in enumerate(xpeers):
        w.send(KB, kblock(yh, yl, x), s_x.at[0, i], r_x.at[x, yh, yl], yl * X + xx, f)
    far = (z + 4) % Z
    for e in range(YH):
        yy = (yh + e) % YH
        recv(H.at[pl.ds(0, half), lanes(far * YH + yy)], r_h.at[far * YH + yy])
        recv(H.at[pl.ds(half, half), lanes(far * YH + yy)], r_h2.at[yy])
    gain(far)
    w.send(QP.at[o], QR, s_q, r_q, s, mate)

    for e, (yy, ll) in enumerate(ypeers):
        block = kblock(yy, ll, x)
        recv(block, r_b.at[yy, ll])
        for i, xx in enumerate(xpeers):
            w.send(block, block, s_x.at[e + 1, i], r_x.at[x, yy, ll], yl * X + xx, f)
    for ll in range(YL):
        part = KVT.at[:, :, :, c, :, lanes(ll * X + x, ROWS)]
        w.send(part, part, s_c.at[0, ll], r_c.at[x, ll], s, mate)
    recv(QR, r_q)
    q = QP[c] + QR[...]
    q1, q2 = q[:64], q[64:]
    co, si = COS[...], SIN[...]
    qt = jnp.concatenate([q1 * co - q2 * si, q2 * co + q1 * si], axis=0)
    QB[...] = jnp.transpose(qt).astype(BF16)
    for i, xx in enumerate(xpeers):
        for ll in range(YL):
            for yy in range(YH):
                recv(kblock(yy, ll, xx), r_x.at[xx, yy, ll])
            part = KVT.at[:, :, :, c, :, lanes(ll * X + xx, ROWS)]
            w.send(part, part, s_c.at[i + 1, ll], r_c.at[xx, ll], s, mate)
    for xx in range(X):
        for ll in range(YL):
            recv(KVT.at[:, :, :, o, :, lanes(ll * X + xx, ROWS)], r_c.at[xx, ll])

    kt = KVT[0].reshape(HD, SEQ)
    vt = KVT[1].reshape(HD, SEQ)
    CH = 64

    def chunk(i, _):
        rows = pl.ds(pl.multiple_of(i * CH, CH), CH)
        raw = nn(QB[rows, :], KVT[0].reshape(HD, SEQ)) * SCALE
        t = s * ROWS + i * CH + lax.broadcasted_iota(jnp.int32, (CH, 1), 0)
        start = openings(t, doc)
        j = lax.broadcasted_iota(jnp.int32, (CH, SEQ), 1)
        raw = jnp.where((j >= start) & (j <= t), raw, -jnp.inf)
        top = jnp.max(raw, axis=1, keepdims=True)
        e = jnp.exp(raw - top)
        probs = (e * (1.0 / jnp.sum(e, axis=1, keepdims=True))).astype(BF16)
        PB[rows, :] = probs
        att_out[rows, :] = nt(probs, KVT[1].reshape(HD, SEQ)).astype(BF16)
        return 0
    lax.fori_loop(0, ROWS // CH, chunk, 0)

    att = att_out[...]
    da = dat[...]
    row_up = nn(pick, da)
    row_dot = jnp.sum(row_up * nn(pick, att), axis=1, keepdims=True)
    row_dp = nn(row_up.astype(BF16), vt)
    row_ds = (nn(pick, PB[...]) * (row_dp - row_dot)).astype(BF16)
    QG[c] = back(nt(row_ds, kt) * SCALE).astype(BF16)
    w.send(QG.at[c], QG.at[c], s_g, r_g, s, mate)
    rowdot = jnp.sum(da.astype(F32) * att.astype(F32), axis=1, keepdims=True)
    colp = nn(PB[...], CM[...])
    cv = nn(vt, CM[...]).astype(BF16)
    cds = (colp * (nn(da, cv) - rowdot)).astype(BF16)
    GP[0] = tn(cds, QB[...]).reshape(YL, X, PL, HD)
    GP[1] = tn(colp.astype(BF16), da).reshape(YL, X, PL, HD)
    w.send(GP.at[o], GR, s_d1, r_d1, s, mate)

    recv(QG.at[o], r_g)
    both = jnp.concatenate([QG[0], QG[1]], axis=1)

    def spread(zz, _):
        part = nn(both, W2[:, pl.ds(pl.multiple_of(zz * 512, 512), 512)])
        for yy in range(YH):
            QF[yy, zz] = part[:, yy * 128:(yy + 1) * 128].astype(BF16)
        QS[zz] = jnp.zeros((PL, HD), F32)
        for yy in range(YH):
            QS[zz] = QS[zz] + jnp.where(yy == yh, part[:, yy * 128:(yy + 1) * 128], 0.0)
        return 0
    lax.fori_loop(0, Z, spread, 0)

    recv(GR, r_d1)
    G1[...] = GP[c] + GR[...]
    for e, xx in enumerate(xpeers):
        w.send(G1.at[:, xx], GX.at[x], s_d2.at[e], r_d2.at[x], yl * X + xx, f)
    for e in range(1, YH):
        yy = (yh + e) % YH
        w.send(QF.at[yy], QY.at[yh], s_e2.at[e - 1], r_e2.at[yh], s, d.fid(z, yy, c))
    acc = G1[:, x]
    for xx in xpeers:
        recv(GX.at[xx], r_d2.at[xx])
        acc = acc + GX[xx]
    G2[...] = acc
    for e, (yy, ll) in enumerate(ypeers):
        w.send(G2.at[ll], GY.at[yh, yl], s_d3.at[e], r_d3.at[yh, yl], ll * X + x, d.fid(z, yy, c))
    for e in range(1, YH):
        yy = (yh + e) % YH
        recv(QY.at[yy], r_e2.at[yy])
        QS[...] = QS[...] + QY[yy].astype(F32)
    for e, zz in enumerate(zpeers):
        w.send(QS.at[zz], QZ.at[z], s_e3.at[e], r_e3.at[z], s, d.fid(zz, yh, c))
    acc = G2[yl]
    for yy, ll in ypeers:
        recv(GY.at[yy, ll], r_d3.at[yy, ll])
        acc = acc + GY[yy, ll]
    dkv = jnp.where(c == 0, back(acc * SCALE), acc).astype(BF16)
    DK[...] = dkv
    DKV[z, c] = dkv
    w.send(DK, DKV.at[z, c], s_d4.at[Z - 1, 0], r_d4.at[z, c], s, mate)
    for e, zz in enumerate(zpeers):
        for i, cc in enumerate((c, o)):
            w.send(DK, DKV.at[z, c], s_d4.at[e, i], r_d4.at[z, c], s, d.fid(zz, yh, cc))
    out = QS[z]
    for zz in zpeers:
        recv(QZ.at[zz], r_e3.at[zz])
        out = out + QZ[zz]
    kvload.wait()
    recv(DKV.at[z, o], r_d4.at[z, o])
    for zz in zpeers:
        recv(DKV.at[zz, 0], r_d4.at[zz, 0])
        recv(DKV.at[zz, 1], r_d4.at[zz, 1])
    wide = jnp.concatenate([DKV[g, p] for g in range(Z) for p in range(2)], axis=1)
    pg_out[...] = out + nn(wide, KVL[...])
    w.finish()


def per_device(hidden, q_weight, kv_weight, d_attended, doc_lengths, prompt_pos):
    vm = pl.BlockSpec(memory_space=pltpu.VMEM)
    anyspace = pl.BlockSpec(memory_space=pl.ANY)
    smem = pl.BlockSpec(memory_space=pltpu.SMEM)
    return pl.pallas_call(
        whole,
        out_shape=(jax.ShapeDtypeStruct((ROWS, HD), BF16),
                   jax.ShapeDtypeStruct((PL, HD), F32)),
        in_specs=[vm, anyspace, anyspace, anyspace, vm, smem, vm],
        out_specs=(vm, vm),
        scratch_shapes=[
            VMEM((ROWS, 4096), BF16),
            VMEM((256, 4096), BF16),
            VMEM((Z, 2, 32, 512), BF16),
            VMEM((2, Z, 2, 16, ROWS), F32),
            VMEM((Z, 2, 16, ROWS), F32),
            VMEM((Z, 2, 16, ROWS), F32),
            VMEM((Z, 2, 16, ROWS), F32),
            VMEM((2, 16, ROWS), BF16),
            VMEM((2, HD, ROWS), F32),
            VMEM((HD, ROWS), F32),
            VMEM((2, 2, 2, 2, 16, SEQ), BF16),
            VMEM((HD // 2, ROWS), F32),
            VMEM((HD // 2, ROWS), F32),
            VMEM((ROWS, HD), BF16),
            VMEM((ROWS, SEQ), BF16),
            VMEM((SEQ, NP), BF16),
            VMEM((SEQ, FB), BF16),
            VMEM((2, PL, HD), BF16),
            VMEM((2, YL, X, PL, HD), F32),
            VMEM((YL, X, PL, HD), F32),
            VMEM((YL, X, PL, HD), F32),
            VMEM((X, YL, PL, HD), F32),
            VMEM((YL, PL, HD), F32),
            VMEM((YH, YL, PL, HD), F32),
            VMEM((PL, HD), BF16),
            VMEM((Z, 2, PL, HD), BF16),
            VMEM((YH, Z, PL, HD), BF16),
            VMEM((YH, Z, PL, HD), BF16),
            VMEM((Z, PL, HD), F32),
            VMEM((Z, PL, HD), F32),
            DMA((3,)), DMA((Z * YH,)), DMA((YH,)), DMA((2, 4, YH)),
            DMA(()), DMA(()), DMA(()),
            DMA((3,)), DMA((YH,)), DMA(()),
            DMA(()), DMA(()),
            DMA((Z - 1,)), DMA((Z,)),
            DMA((YH * YL - 1,)), DMA((YH, YL)),
            DMA((YH * YL, X - 1)), DMA((X, YH, YL)),
            DMA((X, YL)), DMA((X, YL)),
            DMA(()), DMA(()), DMA(()),
            DMA(()), DMA(()),
            DMA(()), DMA(()),
            DMA((X - 1,)), DMA((X,)),
            DMA((YH * YL - 1,)), DMA((YH, YL)),
            DMA((Z, 2)), DMA((Z, 2)),
            DMA((YH - 1,)), DMA((YH,)),
            DMA((Z - 1,)), DMA((Z,)),
        ],
        compiler_params=pltpu.CompilerParams(
            collective_id=0, has_side_effects=True, vmem_limit_bytes=48 << 20),
        name="whole",
    )(hidden, q_weight, kv_weight.reshape(Z, 2, 2, 2, 32, FB), kv_weight, d_attended,
      doc_lengths, prompt_pos.reshape(1, NP))


def solution(mesh):
    placed = (P("seq", "fsdp"), P("fsdp", None), P(None, "fsdp"), P("seq", "fsdp"), P(), P())
    return jax.shard_map(
        per_device,
        mesh=mesh,
        in_specs=placed,
        out_specs=(P("seq", "fsdp"), P("seq", "fsdp")),
        check_vma=False,
    )
```

time: 730 us -> 97.3 us (0.13)
  blocking collectives: 592 us -> 0 us
  Pallas kernels: 0 us -> 89.5 us
  waiting for transfers between devices: 79.6 us -> 0 us
  matrix products: 14.9 us -> 0 us
  between operations: 14 us -> 0.65 us
  local copies, waits for them, and re-layouts: 17.6 us -> 6.84 us
    psum x2 -> x0, blocking collectives: 592 us -> none  [the longest x1 308 us: per_device(): kv_summed = lax.psum(kv_partial, 'fsdp')]
    pallas_call x0 -> x1, Pallas kernels: none -> 89.5 us  [per_device(): pl.pallas_call(whole, out_shape=(jax.ShapeDtypeStruct((ROWS, HD), BF16),...]
    unnamed x5 -> x0, waiting for transfers between devices: 40.2 us -> none
    all_gather x2 -> x0, waiting for transfers between devices: 39.3 us -> none  [the longest x1 39.3 us: per_device(): kv_full = lax.all_gather(kv_block, 'seq', axis=0, tiled=True)]
    dot_general x9 -> x0, matrix products: 14.9 us -> none  [the longest x1 3.72 us: per_device(): lax.dot_general(lax.all_gather(hidden, 'fsdp', axis=1, tiled=True), q_wei...]
    gather x7 -> x0, local copies, waits for them, and re-layouts: 8.54 us -> none  [the longest x1 2.54 us: per_device(): col_values = value_blocks[block_of, column_of]]
  transfers between devices with their start and end apart: 4 -> 0, of which waited for: 2 -> 0; matrix products, arithmetic and copies ran while one was open for 2% -> 0% of each run, Pallas kernels for 0% -> 0%
where the time goes in v1:
time: 97.3 us; the launch traced here: 97 us
  Pallas kernels  89.5 us (92%)
  local copies, waits for them, and re-layouts  6.84 us (7%)
    pallas_call x1, Pallas kernels, per_device(): pl.pallas_call(whole, out_shape=(jax.ShapeDtypeStruct((ROWS, HD), BF16),...  89.5 us
    unnamed x14, local copies, waits for them, and re-layouts  6.84 us

profile of v1, /device:TPU:1, one launch (start us, length us, event | category | flops | bytes accessed | tf_op | source)
XLA Modules:
  0.0 97.0 jit_solution(4816038416853146748)
XLA Ops:
  0.6 0.0 copy-start
  0.6 1.6 %copy-done = bf16[128,8192]{1,0:T(8,128)(2,1)S(1)} copy-done((bf16[128,8192]{1,0:T(8,128)(2,1)S(1)}, bf16[128,8192]{1,0:T(8,128)(2,1)}, u32[]{:S(2)}) %copy-start) | copy-done | bytes 2097176
  2.2 0.0 copy-start.1
  2.2 1.0 %copy-done.1 = bf16[2048,128]{1,0:T(8,128)(2,1)S(1)} copy-done((bf16[2048,128]{1,0:T(8,128)(2,1)S(1)}, bf16[2048,128]{1,0:T(8,128)(2,1)}, u32[]{:S(2)}) %copy-start.1) | copy-done | bytes 524312
  3.3 0.0 copy-start.2
  3.3 0.8 copy-done.2
  4.1 0.0 copy-start.3
  4.1 0.8 copy-done.3
  4.9 0.0 copy-start.4
  4.9 0.7 copy-done.4
  5.6 0.0 copy-start.5
  5.6 0.7 copy-done.5
  6.3 89.5 %whole.1 = (bf16[256,128]{1,0:T(8,128)(2,1)S(1)}, f32[16,128]{1,0:T(8,128)S(1)}) custom-call(bf16[256,128]{1,0:T(8,128)(2,1)S(1)} %copy-done.2, bf16[128,8192]{1,0:T(8,128)(2,1)S(1)} %copy-done, bf16[8,2,2,2,32,128]{5,4,3,2,1,0:T(8,128)(2,1)S(1)} %bitcast.2, bf16[2048,128]{1,0:T(8,128)(2,1)S(1)} %copy-done.1, bf16[256,128]{1,0:T(8,128)(2,1)S(1)} %copy-done.3, ...), custom_call_target="tpu_custom_call" | custom-call | tf_op jit(solution)/shard_map/whole/pallas_call | solution.py:383
  95.8 0.6 copy.10
  96.4 0.6 copy.11
Async XLA Ops:
  0.6 1.6 %copy-start = (bf16[128,8192]{1,0:T(8,128)(2,1)S(1)}, bf16[128,8192]{1,0:T(8,128)(2,1)}, u32[]{:S(2)}) copy-start(bf16[128,8192]{1,0:T(8,128)(2,1)} %qw.1) | copy-start | bytes 6291460
  2.2 1.0 %copy-start.1 = (bf16[2048,128]{1,0:T(8,128)(2,1)S(1)}, bf16[2048,128]{1,0:T(8,128)(2,1)}, u32[]{:S(2)}) copy-start(bf16[2048,128]{1,0:T(8,128)(2,1)} %kvflat.1) | copy-start | bytes 1572868
  3.3 0.8 copy-start.2
  4.1 0.8 copy-start.3
  4.9 0.7 copy-start.4
  5.6 0.7 copy-start.5

commit v2 on v1

--- a/solution.py
+++ b/solution.py
@@ -83,18 +83,22 @@
     return start
 
 
-def whole(hid, qw, kvw, kvflat, dat, doc, prow, att_out, pg_out,
-          H, W2, KW, PS, PR, SS, SR, KB, QP, QR, KVT, COS, SIN, QB, PB, CM, KVL,
-          QG, GP, GR, G1, GX, G2, GY, DK, DKV, QF, QY, QS, QZ,
-          s_h, r_h, r_h2, s_hz, s_w, r_w, l_w, s_k, r_k, l_k, s_p, r_p, s_s, r_s,
-          s_b, r_b, s_x, r_x, s_c, r_c, s_q, r_q, l_v,
-          s_g, r_g, s_d1, r_d1, s_d2, r_d2, s_d3, r_d3, s_d4, r_d4, s_e2, r_e2, s_e3, r_e3):
+def whole(hid, qw, kvw, kvflat, dhbm, dochbm, phbm, att_out, pg_out,
+          H, W2, KZ, KY, KW, KWF, KP, KR, KB, QP, QR, KVT, COS, SIN, QB, PB, CM, KVL,
+          QG, GP, GX, G2, GY, DK, DKV, QF, QY, QS, QZ, dat, doc, prow,
+          s_h, r_h, r_h2, s_hz, s_w, r_w, l_w, s_kz, r_kz, s_ky, r_ky, s_kl, r_kl, s_kx, r_kx,
+          s_p, r_p, s_b, r_b, s_x, r_x, s_c, r_c, s_q, r_q, l_v, l_in,
+          s_g, r_g, s_d2, r_d2, s_d3, r_d3, s_d4, r_d4, s_e2, r_e2, s_e3, r_e3):
     d = Place()
     s, f, x, yl, z, yh, c, o = d.s, d.f, d.x, d.yl, d.z, d.yh, d.c, d.o
     mate = d.fid(z, yh, o)
     zup, zdn = (z + 1) % Z, (z + Z - 1) % Z
     w = Wires()
 
+    loads = [pltpu.make_async_copy(a, b, l_in.at[i]) for i, (a, b) in enumerate(
+        ((dochbm, doc), (phbm, prow), (dhbm, dat)))]
+    for load in loads:
+        load.start()
     bar = pltpu.get_barrier_semaphore()
     peers = [(s, mate)]
     ypeers = []
@@ -105,6 +109,7 @@
     xpeers = [(x + e) % X for e in range(1, X)]
     for xx in xpeers:
         peers.append((yl * X + xx, f))
+        peers.append((yl * X + xx, mate))
     zpeers = [(z + e) % Z for e in range(1, Z)]
     for zz in zpeers:
         peers.append((s, d.fid(zz, yh, c)))
@@ -116,23 +121,22 @@
     def hblock(zz, yy):
         return H.at[:, lanes(zz * YH + yy)]
 
-    def wslice(yy):
-        return kvw.at[:, yy // 2, :, yy % 2]
-
     def recv(ref, sem):
         w.make(ref, ref, s_q, sem, s, mate).wait_recv()
 
+    def eighth(g):
+        return kvw.at[g, :, s // 4, :, pl.ds(pl.multiple_of((s % 4) * 8, 8), 8), :]
+    for e, zz in enumerate(zpeers):
+        w.send(eighth(zz), KZ.at[z], s_kz.at[e], r_kz.at[z], s, d.fid(zz, yh, c))
+    kzown = pltpu.make_async_copy(eighth(z), KZ.at[z], l_in.at[3])
+    kzown.start()
+    hown = pltpu.make_async_copy(hid, hblock(z, yh), l_in.at[4])
+    hown.start()
     for e in range(1, YH):
         yy = (yh + e) % YH
         w.send(hid, hblock(z, yh), s_h.at[e - 1], r_h.at[z * YH + yh], s, d.fid(z, yy, c))
     for i, zz in enumerate((zup, zdn)):
         w.send(hid, hblock(z, yh), s_hz.at[i, 0, 0], r_h.at[z * YH + yh], s, d.fid(zz, yh, c))
-    for e in range(1, YH):
-        yy = (yh + e) % YH
-        w.send(wslice(yy), KW.at[:, :, :, lanes(yh)], s_k.at[e - 1], r_k.at[yh], s, d.fid(z, yy, c))
-    kown = pltpu.make_async_copy(wslice(yh), KW.at[:, :, :, lanes(yh)], l_k)
-    kown.start()
-
     def wload(k, _):
         pltpu.make_async_copy(qw.at[:, pl.ds(pl.multiple_of(k * 256 + c * 128, 128), 128)],
                               W2.at[pl.ds(c * 128, 128), lanes(k)], l_w).start()
@@ -142,7 +146,8 @@
     lax.fori_loop(0, Z * YH, wload, 0)
     kvload = pltpu.make_async_copy(kvflat, KVL, l_v)
     kvload.start()
-    H[:, lanes(z * YH + yh)] = hid[...]
+    for load in loads:
+        load.wait()
 
     tok = s * ROWS + lax.broadcasted_iota(jnp.int32, (1, ROWS), 1)
     place = (tok - openings(tok, doc)).astype(F32)
@@ -199,42 +204,68 @@
         QP[0] = QP[0] + part[:128]
         QP[1] = QP[1] + part[128:]
 
+    def gain_kv(zz):
+        cols = pl.ds(pl.multiple_of(zz * 512, 512), 512)
+        part = nt(KWF[:, cols], H[:, cols]).reshape(2, 2, 16, ROWS)
+        KP[0] = KP[0] + part[:, 0]
+        KP[1] = KP[1] + part[:, 1]
+
+    kzown.wait()
+    for zz in zpeers:
+        recv(KZ.at[zz], r_kz.at[zz])
+    for e in range(1, YH):
+        yy = (yh + e) % YH
+        w.send(KZ.at[:, yy // 2, yy % 2], KY.at[yh], s_ky.at[e - 1], r_ky.at[yh], s, d.fid(z, yy, c))
+    KY[yh] = KZ[:, yh // 2, yh % 2]
     forward(0)
+    for e in range(1, YH):
+        yy = (yh + e) % YH
+        recv(KY.at[yy], r_ky.at[yy])
+    for zz in range(Z):
+        for yy in range(YH):
+            KW[s, :, pl.ds((zz * YH + yy) * 128, 128)] = KY[yy, zz]
+    sx = (1 - yl) * X + x
+    w.send(KW.at[s], KW.at[s], s_kl, r_kl, sx, f)
     mine_w, other_w = W2.at[pl.ds(c * 128, 128)], W2.at[pl.ds(o * 128, 128)]
     pltpu.make_async_copy(mine_w, mine_w, l_w).wait()
     recv(other_w, r_w)
     w.make(other_w, other_w, s_w, r_w, s, mate).wait_send()
+    hown.wait()
     QP[...] = jnp.zeros_like(QP)
+    KP[...] = jnp.zeros_like(KP)
     gain(z)
     forward(1)
+    recv(KW.at[sx], r_kl)
+    for i, xx in enumerate(xpeers):
+        for ll in range(YL):
+            w.send(KW.at[ll * X + x], KW.at[ll * X + x], s_kx.at[i, ll], r_kx.at[x, ll], yl * X + xx, f)
     gain((z + 1) % Z)
     gain((z + Z - 1) % Z)
     forward(2)
     gain((z + 2) % Z)
     gain((z + Z - 2) % Z)
-    kown.wait()
-    for e in range(1, YH):
-        yy = (yh + e) % YH
-        recv(KW.at[:, :, :, lanes(yy)], r_k.at[yy])
-    mine = pl.ds(pl.multiple_of(z * 512, 512), 512)
-    for g in range(Z):
-        part = nt(KW[g].reshape(64, 512), H[:, mine]).reshape(2, 2, 16, ROWS)
-        PS[0, g] = part[:, 0]
-        PS[1, g] = part[:, 1]
-    w.send(PS.at[o], PR, s_p, r_p, s, mate)
     forward(3)
-    recv(PR, r_p)
-    SS[...] = PS[c] + PR[...]
-    for e, zz in enumerate(zpeers):
-        w.send(SS.at[zz], SR.at[z], s_s.at[e], r_s.at[z], s, d.fid(zz, yh, c))
-    SR[z] = SS[z]
     gain((z + 3) % Z)
     gain((z + Z - 3) % Z)
-    for zz in zpeers:
-        recv(SR.at[zz], r_s.at[zz])
-    total = SR[0]
-    for i in range(1, Z):
-        total = total + SR[i]
+    for xx in xpeers:
+        for ll in range(YL):
+            recv(KW.at[ll * X + xx], r_kx.at[xx, ll])
+    for i in range(X * YL):
+        KWF[pl.ds(i * 8, 8), :] = KW[i]
+    for i in range(Z):
+        if i != 4:
+            gain_kv((z + i) % Z)
+    far = (z + 4) % Z
+    for e in range(YH):
+        yy = (yh + e) % YH
+        recv(H.at[pl.ds(0, half), lanes(far * YH + yy)], r_h.at[far * YH + yy])
+        recv(H.at[pl.ds(half, half), lanes(far * YH + yy)], r_h2.at[yy])
+    gain_kv(far)
+    w.send(KP.at[o], KR, s_p, r_p, s, mate)
+    gain(far)
+    w.send(QP.at[o], QR, s_q, r_q, s, mate)
+    recv(KR, r_p)
+    total = KP[c] + KR[...]
     kvb = total.astype(BF16)
     kf = kvb.astype(F32)
     b16 = pl.ds(pl.multiple_of((yh % 2) * 32 + c * 16, 16), 16)
@@ -251,14 +282,6 @@
     KVT[yh // 2, :, yh % 2, c, :, lanes(s, ROWS)] = KB[...]
     for i, xx in enumerate(xpeers):
         w.send(KB, kblock(yh, yl, x), s_x.at[0, i], r_x.at[x, yh, yl], yl * X + xx, f)
-    far = (z + 4) % Z
-    for e in range(YH):
-        yy = (yh + e) % YH
-        recv(H.at[pl.ds(0, half), lanes(far * YH + yy)], r_h.at[far * YH + yy])
-        recv(H.at[pl.ds(half, half), lanes(far * YH + yy)], r_h2.at[yy])
-    gain(far)
-    w.send(QP.at[o], QR, s_q, r_q, s, mate)
-
     for e, (yy, ll) in enumerate(ypeers):
         block = kblock(yy, ll, x)
         recv(block, r_b.at[yy, ll])
@@ -304,20 +327,23 @@
 
     att = att_out[...]
     da = dat[...]
+    rowdot = jnp.sum(da.astype(F32) * att.astype(F32), axis=1, keepdims=True)
+    colp = nn(PB[...], CM[...])
+    cv = nn(vt, CM[...]).astype(BF16)
+    cds = (colp * (nn(da, cv) - rowdot)).astype(BF16)
+    GP[0] = tn(cds, QB[...]).reshape(YL, X, PL, HD)
+    GP[1] = tn(colp.astype(BF16), da).reshape(YL, X, PL, HD)
+    for e in range(X):
+        xx = (x + e) % X
+        for i, (pp, ff) in enumerate(((c, f), (o, mate))):
+            if e or i:
+                w.send(GP.at[pp, :, xx], GX.at[x, c], s_d2.at[e, i], r_d2.at[x, c], yl * X + xx, ff)
     row_up = nn(pick, da)
     row_dot = jnp.sum(row_up * nn(pick, att), axis=1, keepdims=True)
     row_dp = nn(row_up.astype(BF16), vt)
     row_ds = (nn(pick, PB[...]) * (row_dp - row_dot)).astype(BF16)
     QG[c] = back(nt(row_ds, kt) * SCALE).astype(BF16)
     w.send(QG.at[c], QG.at[c], s_g, r_g, s, mate)
-    rowdot = jnp.sum(da.astype(F32) * att.astype(F32), axis=1, keepdims=True)
-    colp = nn(PB[...], CM[...])
-    cv = nn(vt, CM[...]).astype(BF16)
-    cds = (colp * (nn(da, cv) - rowdot)).astype(BF16)
-    GP[0] = tn(cds, QB[...]).reshape(YL, X, PL, HD)
-    GP[1] = tn(colp.astype(BF16), da).reshape(YL, X, PL, HD)
-    w.send(GP.at[o], GR, s_d1, r_d1, s, mate)
-
     recv(QG.at[o], r_g)
     both = jnp.concatenate([QG[0], QG[1]], axis=1)
 
@@ -331,17 +357,15 @@
         return 0
     lax.fori_loop(0, Z, spread, 0)
 
-    recv(GR, r_d1)
-    G1[...] = GP[c] + GR[...]
-    for e, xx in enumerate(xpeers):
-        w.send(G1.at[:, xx], GX.at[x], s_d2.at[e], r_d2.at[x], yl * X + xx, f)
     for e in range(1, YH):
         yy = (yh + e) % YH
         w.send(QF.at[yy], QY.at[yh], s_e2.at[e - 1], r_e2.at[yh], s, d.fid(z, yy, c))
-    acc = G1[:, x]
+    recv(GX.at[x, o], r_d2.at[x, o])
+    acc = GP[c, :, x] + GX[x, o]
     for xx in xpeers:
-        recv(GX.at[xx], r_d2.at[xx])
-        acc = acc + GX[xx]
+        for cc in range(C):
+            recv(GX.at[xx, cc], r_d2.at[xx, cc])
+            acc = acc + GX[xx, cc]
     G2[...] = acc
     for e, (yy, ll) in enumerate(ypeers):
         w.send(G2.at[ll], GY.at[yh, yl], s_d3.at[e], r_d3.at[yh, yl], ll * X + x, d.fid(z, yy, c))
@@ -378,22 +402,22 @@
 
 def per_device(hidden, q_weight, kv_weight, d_attended, doc_lengths, prompt_pos):
     vm = pl.BlockSpec(memory_space=pltpu.VMEM)
-    anyspace = pl.BlockSpec(memory_space=pl.ANY)
-    smem = pl.BlockSpec(memory_space=pltpu.SMEM)
+    hbm = pl.BlockSpec(memory_space=pltpu.HBM)
     return pl.pallas_call(
         whole,
         out_shape=(jax.ShapeDtypeStruct((ROWS, HD), BF16),
                    jax.ShapeDtypeStruct((PL, HD), F32)),
-        in_specs=[vm, anyspace, anyspace, anyspace, vm, smem, vm],
+        in_specs=[hbm] * 7,
         out_specs=(vm, vm),
         scratch_shapes=[
             VMEM((ROWS, 4096), BF16),
             VMEM((256, 4096), BF16),
-            VMEM((Z, 2, 32, 512), BF16),
-            VMEM((2, Z, 2, 16, ROWS), F32),
-            VMEM((Z, 2, 16, ROWS), F32),
-            VMEM((Z, 2, 16, ROWS), F32),
-            VMEM((Z, 2, 16, ROWS), F32),
+            VMEM((Z, 2, 2, 8, FB), BF16),
+            VMEM((YH, Z, 8, FB), BF16),
+            VMEM((X * YL, 8, 4096), BF16),
+            VMEM((64, 4096), BF16),
+            VMEM((2, 2, 16, ROWS), F32),
+            VMEM((2, 16, ROWS), F32),
             VMEM((2, 16, ROWS), BF16),
             VMEM((2, HD, ROWS), F32),
             VMEM((HD, ROWS), F32),
@@ -406,9 +430,7 @@
             VMEM((SEQ, FB), BF16),
             VMEM((2, PL, HD), BF16),
             VMEM((2, YL, X, PL, HD), F32),
-            VMEM((YL, X, PL, HD), F32),
-            VMEM((YL, X, PL, HD), F32),
-            VMEM((X, YL, PL, HD), F32),
+            VMEM((X, C, YL, PL, HD), F32),
             VMEM((YL, PL, HD), F32),
             VMEM((YH, YL, PL, HD), F32),
             VMEM((PL, HD), BF16),
@@ -417,25 +439,27 @@
             VMEM((YH, Z, PL, HD), BF16),
             VMEM((Z, PL, HD), F32),
             VMEM((Z, PL, HD), F32),
+            VMEM((ROWS, FB), BF16),
+            pltpu.SMEM((4,), jnp.int32),
+            VMEM((1, NP), jnp.int32),
             DMA((3,)), DMA((Z * YH,)), DMA((YH,)), DMA((2, 4, YH)),
             DMA(()), DMA(()), DMA(()),
-            DMA((3,)), DMA((YH,)), DMA(()),
+            DMA((Z - 1,)), DMA((Z,)), DMA((YH - 1,)), DMA((YH,)),
+            DMA(()), DMA(()), DMA((X - 1, YL)), DMA((X, YL)),
             DMA(()), DMA(()),
-            DMA((Z - 1,)), DMA((Z,)),
             DMA((YH * YL - 1,)), DMA((YH, YL)),
             DMA((YH * YL, X - 1)), DMA((X, YH, YL)),
             DMA((X, YL)), DMA((X, YL)),
-            DMA(()), DMA(()), DMA(()),
+            DMA(()), DMA(()), DMA(()), DMA((5,)),
             DMA(()), DMA(()),
-            DMA(()), DMA(()),
-            DMA((X - 1,)), DMA((X,)),
+            DMA((X, C)), DMA((X, C)),
             DMA((YH * YL - 1,)), DMA((YH, YL)),
             DMA((Z, 2)), DMA((Z, 2)),
             DMA((YH - 1,)), DMA((YH,)),
             DMA((Z - 1,)), DMA((Z,)),
         ],
         compiler_params=pltpu.CompilerParams(
-            collective_id=0, has_side_effects=True, vmem_limit_bytes=48 << 20),
+            collective_id=0, has_side_effects=True, vmem_limit_bytes=67043328),
         name="whole",
     )(hidden, q_weight, kv_weight.reshape(Z, 2, 2, 2, 32, FB), kv_weight, d_attended,
       doc_lengths, prompt_pos.reshape(1, NP))

time: 97.3 us -> 86.9 us (0.89)
  Pallas kernels: 89.5 us -> 83.3 us
  local copies, waits for them, and re-layouts: 6.84 us -> 2.77 us
    pallas_call x1, Pallas kernels: 89.5 us -> 83.3 us  [per_device(): pl.pallas_call(whole, out_shape=(jax.ShapeDtypeStruct((ROWS, HD), BF16),...]
    unnamed x14 -> x2, local copies, waits for them, and re-layouts: 6.84 us -> 2.77 us
where the time goes in v2:
time: 86.9 us; the launch traced here: 86.7 us
  Pallas kernels  83.3 us (96%)
  local copies, waits for them, and re-layouts  2.77 us (3%)
    pallas_call x1, Pallas kernels, per_device(): pl.pallas_call(whole, out_shape=(jax.ShapeDtypeStruct((ROWS, HD), BF16),...  83.3 us
    unnamed x2, local copies, waits for them, and re-layouts  2.77 us

profile of v2, /device:TPU:1, one launch (start us, length us, event | category | flops | bytes accessed | tf_op | source)
XLA Modules:
  0.0 86.7 jit_solution(5483685460782345894)
XLA Ops:
  0.6 83.3 %whole.1 = (bf16[256,128]{1,0:T(8,128)(2,1)}, f32[16,128]{1,0:T(8,128)}) custom-call(bf16[256,128]{1,0:T(8,128)(2,1)} %hid.1, bf16[128,8192]{1,0:T(8,128)(2,1)} %qw.1, bf16[8,2,2,2,32,128]{5,4,3,2,1,0:T(8,128)(2,1)} %bitcast.2, bf16[2048,128]{1,0:T(8,128)(2,1)} %kvflat.1, bf16[256,128]{1,0:T(8,128)(2,1)} %dhbm.1, s32[4]{0:T(128)} %dochbm.1, s32[1,128]{1,0:T(1,128)} %bitcast.3), custom_call_target="tpu_custom_call" | custom-call | tf_op jit(solution)/shard_map/whole/pallas_call | solution.py:406
  83.9 1.5 %copy.10 = bf16[256,128]{1,0:T(8,128)(2,1)} copy(bf16[256,128]{1,0:T(8,128)(2,1)} %get-tuple-element.4) | data formatting | bytes 131072
  85.4 1.3 %copy.11 = f32[16,128]{1,0:T(8,128)} copy(f32[16,128]{1,0:T(8,128)} %get-tuple-element.5) | data formatting | bytes 16384

commit v3 on v2

--- a/solution.py
+++ b/solution.py
@@ -65,6 +65,57 @@
     return lax.dot_general(a, b, (((0,), (0,)), ((), ())), preferred_element_type=F32)
 
 
+class Flow:
+    RATE = {"z+": 45.0, "z-": 45.0, "y+": 22.0, "y-": 22.0, "x+": 45.0, "x-": 45.0, "m": 300.0, "n": 1e9}
+    LAG = {"z+": 1.7, "z-": 1.7, "y+": 2.5, "y-": 2.5, "x+": 1.7, "x-": 1.7, "m": 0.9, "n": 4.0}
+
+    def __init__(self):
+        self.tasks = {}
+        self.recvs = {}
+
+    def arrival(self, key, ref, sem):
+        self.recvs[key] = (ref, sem)
+
+    def task(self, name, needs=(), after=(), sends=(), work=None, cost=0.05, rank=0):
+        self.tasks[name] = (set(needs), set(after), list(sends), work, cost, rank)
+
+    def order(self):
+        at, done, free, now, out = {}, {}, {}, 0.0, []
+        todo = list(self.tasks)
+        while todo:
+            best = None
+            for i, name in enumerate(todo):
+                needs, after, _, _, _, rank = self.tasks[name]
+                if all(n in at for n in needs) and all(a in done for a in after):
+                    ready = max([at[n] for n in needs] + [done[a] for a in after] + [0.0])
+                    cand = (max(ready, now), rank, i)
+                    if best is None or cand < best:
+                        best = cand
+            assert best is not None, todo
+            name = todo.pop(best[2])
+            _, _, sends, _, cost, _ = self.tasks[name]
+            now = best[0] + cost
+            done[name] = now
+            for link, size, key, _ in sends:
+                start = max(free.get(link, 0.0), now)
+                free[link] = start + size / self.RATE[link]
+                if key is not None:
+                    at[key] = max(at.get(key, 0.0), free[link] + self.LAG[link])
+            out.append(name)
+        self.model = done
+        return out
+
+    def emit(self, recv):
+        for name in self.order():
+            needs, _, sends, work, _, _ = self.tasks[name]
+            for key in sorted(needs, key=repr):
+                recv(*self.recvs[key])
+            if work is not None:
+                work()
+            for _, _, _, go in sends:
+                go()
+
+
 def lanes(k, n=128):
     return pl.ds(pl.multiple_of(k * n, n), n)
 
@@ -86,7 +137,7 @@
 def whole(hid, qw, kvw, kvflat, dhbm, dochbm, phbm, att_out, pg_out,
           H, W2, KZ, KY, KW, KWF, KP, KR, KB, QP, QR, KVT, COS, SIN, QB, PB, CM, KVL,
           QG, GP, GX, G2, GY, DK, DKV, QF, QY, QS, QZ, dat, doc, prow,
-          s_h, r_h, r_h2, s_hz, s_w, r_w, l_w, s_kz, r_kz, s_ky, r_ky, s_kl, r_kl, s_kx, r_kx,
+          s_h, r_h, s_w, r_w, l_w, s_kz, r_kz, s_ky, r_ky, s_kl, r_kl, s_kx, r_kx,
           s_p, r_p, s_b, r_b, s_x, r_x, s_c, r_c, s_q, r_q, l_v, l_in,
           s_g, r_g, s_d2, r_d2, s_d3, r_d3, s_d4, r_d4, s_e2, r_e2, s_e3, r_e3):
     d = Place()
@@ -132,71 +183,110 @@
     kzown.start()
     hown = pltpu.make_async_copy(hid, hblock(z, yh), l_in.at[4])
     hown.start()
-    for e in range(1, YH):
-        yy = (yh + e) % YH
-        w.send(hid, hblock(z, yh), s_h.at[e - 1], r_h.at[z * YH + yh], s, d.fid(z, yy, c))
-    for i, zz in enumerate((zup, zdn)):
-        w.send(hid, hblock(z, yh), s_hz.at[i, 0, 0], r_h.at[z * YH + yh], s, d.fid(zz, yh, c))
-    def wload(k, _):
-        pltpu.make_async_copy(qw.at[:, pl.ds(pl.multiple_of(k * 256 + c * 128, 128), 128)],
-                              W2.at[pl.ds(c * 128, 128), lanes(k)], l_w).start()
-        w.make(qw.at[:, pl.ds(pl.multiple_of(k * 256 + o * 128, 128), 128)],
-               W2.at[pl.ds(c * 128, 128), lanes(k)], s_w, r_w, s, mate).start()
-        return 0
-    lax.fori_loop(0, Z * YH, wload, 0)
-    kvload = pltpu.make_async_copy(kvflat, KVL, l_v)
-    kvload.start()
-    for load in loads:
-        load.wait()
-
-    tok = s * ROWS + lax.broadcasted_iota(jnp.int32, (1, ROWS), 1)
-    place = (tok - openings(tok, doc)).astype(F32)
-    freq = jnp.exp(lax.broadcasted_iota(jnp.int32, (HD // 2, 1), 0).astype(F32) * STEP)
-    angle = freq * place
-    COS[...] = jnp.cos(angle)
-    SIN[...] = jnp.sin(angle)
-    prompts = prow[...]
-    for i in range(8):
-        at = i * 256 + lax.broadcasted_iota(jnp.int32, (256, NP), 0)
-        CM[pl.ds(i * 256, 256), :] = jnp.where(at == prompts, 1.0, 0.0).astype(BF16)
-    near = lax.broadcasted_iota(jnp.int32, (PL, NP), 1) == (
-        s * PL + lax.broadcasted_iota(jnp.int32, (PL, NP), 0))
-    own_p = jnp.sum(jnp.where(near, prompts.astype(F32), 0.0), axis=1, keepdims=True).astype(jnp.int32)
-    pick = jnp.where(lax.broadcasted_iota(jnp.int32, (PL, ROWS), 1) == own_p - s * ROWS,
-                     1.0, 0.0).astype(BF16)
-    lane = lax.broadcasted_iota(jnp.int32, (1, HD), 1)
-    freq_l = jnp.exp(jnp.where(lane < 64, lane, lane - 64).astype(F32) * STEP)
-    angle_p = (own_p - openings(own_p, doc)).astype(F32) * freq_l
-    cos_p = jnp.cos(angle_p)
-    sin_p = jnp.where(lane < 64, 1.0, -1.0) * jnp.sin(angle_p)
+    flow = Flow()
+    used = [0]
+    ROW = {"Y": {"F": (0, 192), "A": (0, 96), "B": (96, 96)},
+           "Z": {"F": (192, 64), "A": (192, 32), "B": (224, 32)}}
+
+    def hpiece(kind, dz, dy, h):
+        r0, n = ROW[kind][h]
+        return H.at[pl.ds(r0, n), lanes((z + dz) % Z * YH + (yh + dy) % YH)]
+
+    def hsem(kind, dz, dy, h):
+        return r_h.at[0 if kind == "Y" else 1, 1 if h == "B" else 0, (z + dz) % Z * YH + (yh + dy) % YH]
+
+    def hsend(kind, dz, dy, h, way):
+        ez, ey = {"z+": (1, 0), "z-": (-1, 0), "y+": (0, 1), "y-": (0, -1)}[way]
+        r0, n = ROW[kind][h]
+        slot = s_h.at[used[0]]
+        used[0] += 1
+        src = hid.at[pl.ds(r0, n), :] if (dz, dy) == (0, 0) else hpiece(kind, dz, dy, h)
+
+        def go():
+            w.send(src, hpiece(kind, dz, dy, h), slot, hsem(kind, dz, dy, h),
+                   s, d.fid((z + ez) % Z, (yh + ey) % YH, c))
+        return (way, n / 4, (kind, (dz - ez) % Z, (dy - ey) % YH, h), go)
+
+    def hidden_tasks():
+        for kind in "YZ":
+            for dz in range(Z):
+                for dy in range(YH):
+                    two = dy == 2 and (kind == "Z" or dz == 0) or dz == 4 and (kind == "Y" or dy == 0)
+                    needs = [(kind, dz, dy, h) for h in ("AB" if two else "F")] if dz or dy else []
+                    for key in needs:
+                        flow.arrival(key, hpiece(*key), hsem(*key))
+                    sends = []
+                    if kind == "Y":
+                        if dz == 0:
+                            if dy == 0:
+                                sends += [("y+", "F"), ("y-", "F")]
+                            if dy == 3:
+                                sends.append(("y+", "A"))
+                            if dy == 1:
+                                sends.append(("y-", "B"))
+                            sends += [("z+", "F"), ("z-", "F")]
+                        elif dz > 4:
+                            sends.append(("z+", "A" if dz == 5 else "F"))
+                        elif dz < 4:
+                            sends.append(("z-", "B" if dz == 3 else "F"))
+                    elif dy == 0:
+                        if dz == 0:
+                            sends += [("z+", "F"), ("z-", "F")]
+                        elif dz > 4:
+                            sends.append(("z+", "A" if dz == 5 else "F"))
+                        elif dz < 4:
+                            sends.append(("z-", "B" if dz == 3 else "F"))
+                        sends += [("y+", "F"), ("y-", "F")]
+                    elif dy == 3:
+                        sends.append(("y+", "A"))
+                    elif dy == 1:
+                        sends.append(("y-", "B"))
+                    flow.task((kind, dz, dy), needs=needs,
+                              sends=[hsend(kind, dz, dy, h, way) for way, h in sends],
+                              rank=0 if dz or dy else (-2 if kind == "Z" else -1))
+    hidden_tasks()
+
+    T = {}
+
+    def setup():
+        def wload(k, _):
+            pltpu.make_async_copy(qw.at[:, pl.ds(pl.multiple_of(k * 256 + c * 128, 128), 128)],
+                                  W2.at[pl.ds(c * 128, 128), lanes(k)], l_w).start()
+            w.make(qw.at[:, pl.ds(pl.multiple_of(k * 256 + o * 128, 128), 128)],
+                   W2.at[pl.ds(c * 128, 128), lanes(k)], s_w, r_w, s, mate).start()
+            return 0
+        lax.fori_loop(0, Z * YH, wload, 0)
+        kvload = pltpu.make_async_copy(kvflat, KVL, l_v)
+        kvload.start()
+        for load in loads:
+            load.wait()
+
+        tok = s * ROWS + lax.broadcasted_iota(jnp.int32, (1, ROWS), 1)
+        place = (tok - openings(tok, doc)).astype(F32)
+        freq = jnp.exp(lax.broadcasted_iota(jnp.int32, (HD // 2, 1), 0).astype(F32) * STEP)
+        angle = freq * place
+        COS[...] = jnp.cos(angle)
+        SIN[...] = jnp.sin(angle)
+        prompts = prow[...]
+        for i in range(8):
+            at = i * 256 + lax.broadcasted_iota(jnp.int32, (256, NP), 0)
+            CM[pl.ds(i * 256, 256), :] = jnp.where(at == prompts, 1.0, 0.0).astype(BF16)
+        near = lax.broadcasted_iota(jnp.int32, (PL, NP), 1) == (
+            s * PL + lax.broadcasted_iota(jnp.int32, (PL, NP), 0))
+        own_p = jnp.sum(jnp.where(near, prompts.astype(F32), 0.0), axis=1, keepdims=True).astype(jnp.int32)
+        pick = jnp.where(lax.broadcasted_iota(jnp.int32, (PL, ROWS), 1) == own_p - s * ROWS,
+                         1.0, 0.0).astype(BF16)
+        lane = lax.broadcasted_iota(jnp.int32, (1, HD), 1)
+        freq_l = jnp.exp(jnp.where(lane < 64, lane, lane - 64).astype(F32) * STEP)
+        angle_p = (own_p - openings(own_p, doc)).astype(F32) * freq_l
+        cos_p = jnp.cos(angle_p)
+        sin_p = jnp.where(lane < 64, 1.0, -1.0) * jnp.sin(angle_p)
+        T.update(kvload=kvload, pick=pick, cos_p=cos_p, sin_p=sin_p)
 
     def back(u):
-        return u * cos_p + pltpu.roll(u, 64, 1) * sin_p
-
-    half = ROWS // 2
-
-    def forward(step):
-        up, dn = (z + Z - step) % Z, (z + step) % Z
-        for e in range(YH):
-            yy = (yh + e) % YH
-            if step == 0:
-                if e == 0:
-                    continue
-                recv(hblock(z, yy), r_h.at[z * YH + yy])
-                w.send(hblock(z, yy), hblock(z, yy), s_hz.at[0, step, e], r_h.at[z * YH + yy], s, d.fid(zup, yh, c))
-                w.send(hblock(z, yy), hblock(z, yy), s_hz.at[1, step, e], r_h.at[z * YH + yy], s, d.fid(zdn, yh, c))
-            elif step < 3:
-                recv(hblock(up, yy), r_h.at[up * YH + yy])
-                w.send(hblock(up, yy), hblock(up, yy), s_hz.at[0, step, e], r_h.at[up * YH + yy], s, d.fid(zup, yh, c))
-                recv(hblock(dn, yy), r_h.at[dn * YH + yy])
-                w.send(hblock(dn, yy), hblock(dn, yy), s_hz.at[1, step, e], r_h.at[dn * YH + yy], s, d.fid(zdn, yh, c))
-            else:
-                top = H.at[pl.ds(0, half), lanes(up * YH + yy)]
-                recv(hblock(up, yy), r_h.at[up * YH + yy])
-                w.send(top, top, s_hz.at[0, step, e], r_h.at[up * YH + yy], s, d.fid(zup, yh, c))
-                bot = H.at[pl.ds(half, half), lanes(dn * YH + yy)]
-                recv(hblock(dn, yy), r_h.at[dn * YH + yy])
-                w.send(bot, bot, s_hz.at[1, step, e], r_h2.at[yy], s, d.fid(zdn, yh, c))
+        return u * T["cos_p"] + pltpu.roll(u, 64, 1) * T["sin_p"]
+
+    flow.task("setup", after=[("Y", 0, 0)], work=setup, cost=1.0, rank=-1)
 
     def gain(zz):
         cols = pl.ds(pl.multiple_of(zz * 512, 512), 512)
@@ -210,102 +300,157 @@
         KP[0] = KP[0] + part[:, 0]
         KP[1] = KP[1] + part[:, 1]
 
-    kzown.wait()
-    for zz in zpeers:
-        recv(KZ.at[zz], r_kz.at[zz])
-    for e in range(1, YH):
-        yy = (yh + e) % YH
-        w.send(KZ.at[:, yy // 2, yy % 2], KY.at[yh], s_ky.at[e - 1], r_ky.at[yh], s, d.fid(z, yy, c))
-    KY[yh] = KZ[:, yh // 2, yh % 2]
-    forward(0)
-    for e in range(1, YH):
-        yy = (yh + e) % YH
-        recv(KY.at[yy], r_ky.at[yy])
-    for zz in range(Z):
-        for yy in range(YH):
-            KW[s, :, pl.ds((zz * YH + yy) * 128, 128)] = KY[yy, zz]
+    kz_keys = [("kz", i) for i in range(Z - 1)]
+    for key, zz in zip(kz_keys, zpeers):
+        flow.arrival(key, KZ.at[zz], r_kz.at[zz])
+    ysides = [(yh + e) % YH for e in range(1, YH)]
+
+    def ky_go(e, yy):
+        return lambda: w.send(KZ.at[:, yy // 2, yy % 2], KY.at[yh], s_ky.at[e], r_ky.at[yh], s, d.fid(z, yy, c))
+
+    def kz_work():
+        kzown.wait()
+        KY[yh] = KZ[:, yh // 2, yh % 2]
+    flow.task("kz0", sends=[("n", 8, key, lambda: None) for key in kz_keys], rank=-3)
+    flow.task("kz", needs=kz_keys, work=kz_work,
+              sends=[(("y+", "y-", "y+")[e], 16, ("ky", e), ky_go(e, yy)) for e, yy in enumerate(ysides)])
+    for e, yy in enumerate(ysides):
+        flow.arrival(("ky", e), KY.at[yy], r_ky.at[yy])
     sx = (1 - yl) * X + x
-    w.send(KW.at[s], KW.at[s], s_kl, r_kl, sx, f)
-    mine_w, other_w = W2.at[pl.ds(c * 128, 128)], W2.at[pl.ds(o * 128, 128)]
-    pltpu.make_async_copy(mine_w, mine_w, l_w).wait()
-    recv(other_w, r_w)
-    w.make(other_w, other_w, s_w, r_w, s, mate).wait_send()
-    hown.wait()
-    QP[...] = jnp.zeros_like(QP)
-    KP[...] = jnp.zeros_like(KP)
-    gain(z)
-    forward(1)
-    recv(KW.at[sx], r_kl)
-    for i, xx in enumerate(xpeers):
-        for ll in range(YL):
-            w.send(KW.at[ll * X + x], KW.at[ll * X + x], s_kx.at[i, ll], r_kx.at[x, ll], yl * X + xx, f)
-    gain((z + 1) % Z)
-    gain((z + Z - 1) % Z)
-    forward(2)
-    gain((z + 2) % Z)
-    gain((z + Z - 2) % Z)
-    forward(3)
-    gain((z + 3) % Z)
-    gain((z + Z - 3) % Z)
-    for xx in xpeers:
-        for ll in range(YL):
-            recv(KW.at[ll * X + xx], r_kx.at[xx, ll])
-    for i in range(X * YL):
-        KWF[pl.ds(i * 8, 8), :] = KW[i]
-    for i in range(Z):
-        if i != 4:
-            gain_kv((z + i) % Z)
-    far = (z + 4) % Z
-    for e in range(YH):
-        yy = (yh + e) % YH
-        recv(H.at[pl.ds(0, half), lanes(far * YH + yy)], r_h.at[far * YH + yy])
-        recv(H.at[pl.ds(half, half), lanes(far * YH + yy)], r_h2.at[yy])
-    gain_kv(far)
-    w.send(KP.at[o], KR, s_p, r_p, s, mate)
-    gain(far)
-    w.send(QP.at[o], QR, s_q, r_q, s, mate)
-    recv(KR, r_p)
-    total = KP[c] + KR[...]
-    kvb = total.astype(BF16)
-    kf = kvb.astype(F32)
-    b16 = pl.ds(pl.multiple_of((yh % 2) * 32 + c * 16, 16), 16)
-    ck, sk = COS[b16, :], SIN[b16, :]
-    iskey = yh < 2
-    KB[0] = jnp.where(iskey, kf[0] * ck - kf[1] * sk, kf[0]).astype(BF16)
-    KB[1] = jnp.where(iskey, kf[1] * ck + kf[0] * sk, kf[1]).astype(BF16)
+    kx_row = lambda dx, ep: (yl + ep) % YL * X + (x + dx) % X
+
+    def ky_work():
+        for zz in range(Z):
+            for yy in range(YH):
+                KW[s, :, pl.ds((zz * YH + yy) * 128, 128)] = KY[yy, zz]
+
+    def kx_send(dx, ep, way):
+        ex = 1 if way == "x+" else -1
+        row = kx_row(dx, ep)
+        slot = s_kx.at[used[1]]
+        used[1] += 1
+        return (way, 64, ("kx", (dx - ex) % X, ep), lambda: w.send(
+            KW.at[row], KW.at[row], slot, r_kx.at[row], yl * X + (x + ex) % X, f))
+    used.append(0)
+    flow.task("ky", needs=[("ky", e) for e in range(YH - 1)], work=ky_work, cost=0.2,
+              sends=[("y+", 64, ("kl",), lambda: w.send(KW.at[s], KW.at[s], s_kl, r_kl, sx, f)),
+                     kx_send(0, 0, "x+"), kx_send(0, 0, "x-")])
+    flow.arrival(("kl",), KW.at[sx], r_kl)
+    flow.task("kl", needs=[("kl",)], sends=[kx_send(0, 1, "x+"), kx_send(0, 1, "x-")])
+    for ep in range(YL):
+        for dx in range(1, X):
+            flow.arrival(("kx", dx, ep), KW.at[kx_row(dx, ep)], r_kx.at[kx_row(dx, ep)])
+            sends = []
+            if dx == 3 and ep == 0:
+                sends = [kx_send(dx, ep, "x+")]
+            if dx == 1 and ep == 1:
+                sends = [kx_send(dx, ep, "x-")]
+            flow.task(("kx", dx, ep), needs=[("kx", dx, ep)], sends=sends)
+
+    def kwf_work():
+        for i in range(X * YL):
+            KWF[pl.ds(i * 8, 8), :] = KW[i]
+    flow.task("kwf", after=["ky", "kl"] + [("kx", dx, ep) for dx in range(1, X) for ep in range(YL)],
+              work=kwf_work, cost=0.2, rank=1)
+
+    def wq_work():
+        mine_w, other_w = W2.at[pl.ds(c * 128, 128)], W2.at[pl.ds(o * 128, 128)]
+        pltpu.make_async_copy(mine_w, mine_w, l_w).wait()
+        recv(other_w, r_w)
+        w.make(other_w, other_w, s_w, r_w, s, mate).wait_send()
+        hown.wait()
+        QP[...] = jnp.zeros_like(QP)
+        KP[...] = jnp.zeros_like(KP)
+    flow.task("wq0", sends=[("n", 8, ("wq",), lambda: None)], rank=-3)
+    flow.task("wq", after=["wq0", ("Y", 0, 2)], work=wq_work, cost=0.3, rank=1)
+    for dz in range(Z):
+        chunk_of = [(kind, dz, dy) for kind in "YZ" for dy in range(YH)]
+        flow.task(("gkv", dz), after=chunk_of + ["wq", "kwf"], cost=0.15, rank=1,
+                  work=functools.partial(lambda i: gain_kv((z + i) % Z), dz))
+        flow.task(("gq", dz), after=chunk_of + ["wq"], cost=0.32, rank=2,
+                  work=functools.partial(lambda i: gain((z + i) % Z), dz))
+    flow.task("kvx", after=[("gkv", dz) for dz in range(Z)], rank=1,
+              sends=[("m", 32, ("kr",), lambda: w.send(KP.at[o], KR, s_p, r_p, s, mate))])
+    flow.task("qx", after=[("gq", dz) for dz in range(Z)], rank=1,
+              sends=[("m", 128, ("qr",), lambda: w.send(QP.at[o], QR, s_q, r_q, s, mate))])
 
     def kblock(yy, ll, xx):
         return KVT.at[yy // 2, :, yy % 2, c, :, lanes(ll * X + xx, ROWS)]
 
-    for e, (yy, ll) in enumerate(ypeers):
-        w.send(KB, kblock(yh, yl, x), s_b.at[e], r_b.at[yh, yl], ll * X + x, d.fid(z, yy, c))
-    KVT[yh // 2, :, yh % 2, c, :, lanes(s, ROWS)] = KB[...]
-    for i, xx in enumerate(xpeers):
-        w.send(KB, kblock(yh, yl, x), s_x.at[0, i], r_x.at[x, yh, yl], yl * X + xx, f)
-    for e, (yy, ll) in enumerate(ypeers):
-        block = kblock(yy, ll, x)
-        recv(block, r_b.at[yy, ll])
-        for i, xx in enumerate(xpeers):
-            w.send(block, block, s_x.at[e + 1, i], r_x.at[x, yy, ll], yl * X + xx, f)
-    for ll in range(YL):
-        part = KVT.at[:, :, :, c, :, lanes(ll * X + x, ROWS)]
-        w.send(part, part, s_c.at[0, ll], r_c.at[x, ll], s, mate)
-    recv(QR, r_q)
-    q = QP[c] + QR[...]
-    q1, q2 = q[:64], q[64:]
-    co, si = COS[...], SIN[...]
-    qt = jnp.concatenate([q1 * co - q2 * si, q2 * co + q1 * si], axis=0)
-    QB[...] = jnp.transpose(qt).astype(BF16)
-    for i, xx in enumerate(xpeers):
-        for ll in range(YL):
-            for yy in range(YH):
-                recv(kblock(yy, ll, xx), r_x.at[xx, yy, ll])
-            part = KVT.at[:, :, :, c, :, lanes(ll * X + xx, ROWS)]
-            w.send(part, part, s_c.at[i + 1, ll], r_c.at[xx, ll], s, mate)
-    for xx in range(X):
-        for ll in range(YL):
-            recv(KVT.at[:, :, :, o, :, lanes(ll * X + xx, ROWS)], r_c.at[xx, ll])
-
+    def kr_work():
+        total = KP[c] + KR[...]
+        kvb = total.astype(BF16)
+        kf = kvb.astype(F32)
+        b16 = pl.ds(pl.multiple_of((yh % 2) * 32 + c * 16, 16), 16)
+        ck, sk = COS[b16, :], SIN[b16, :]
+        iskey = yh < 2
+        KB[0] = jnp.where(iskey, kf[0] * ck - kf[1] * sk, kf[0]).astype(BF16)
+        KB[1] = jnp.where(iskey, kf[1] * ck + kf[0] * sk, kf[1]).astype(BF16)
+        KVT[yh // 2, :, yh % 2, c, :, lanes(s, ROWS)] = KB[...]
+
+    yrel = [(yh, yl)] + ypeers
+    used.append(0)
+
+    def x_send(dx, e, way):
+        ex = 1 if way == "x+" else -1
+        yy, ll = yrel[e]
+        block = kblock(yy, ll, (x + dx) % X)
+        src = KB if (dx, e) == (0, 0) else block
+        slot = s_x.at[used[2]]
+        used[2] += 1
+        return (way, 16, ("x", (dx - ex) % X, e), lambda: w.send(
+            src, block, slot, r_x.at[(x + dx) % X, yy, ll], yl * X + (x + ex) % X, f))
+
+    def b_send(e):
+        yy, ll = ypeers[e]
+        return ("y+" if e < 4 else "y-", 16 * min(e + 1, 7 - e) / 4, ("b", 7 - e), lambda: w.send(
+            KB, kblock(yh, yl, x), s_b.at[e], r_b.at[yh, yl], ll * X + x, d.fid(z, yy, c)))
+
+    flow.arrival(("kr",), KR, r_p)
+    flow.task("kr", needs=[("kr",)], work=kr_work, cost=0.2,
+              sends=[b_send(e) for e in (3, 2, 4, 1, 5, 0, 6)] + [x_send(0, 0, "x+"), x_send(0, 0, "x-")])
+    for e in range(1, YH * YL):
+        yy, ll = yrel[e]
+        flow.arrival(("b", e), kblock(yy, ll, x), r_b.at[yy, ll])
+        flow.task(("b", e), needs=[("b", e)], sends=[x_send(0, e, "x+"), x_send(0, e, "x-")])
+    for e in range(YH * YL):
+        yy, ll = yrel[e]
+        for dx in range(1, X):
+            xx = (x + dx) % X
+            flow.arrival(("x", dx, e), kblock(yy, ll, xx), r_x.at[xx, yy, ll])
+            sends = []
+            if dx == 3 and e % 2 == 0:
+                sends = [x_send(dx, e, "x+")]
+            if dx == 1 and e % 2 == 1:
+                sends = [x_send(dx, e, "x-")]
+            flow.task(("x", dx, e), needs=[("x", dx, e)], sends=sends)
+
+    def c_send(dx, ep):
+        col = (yl + ep) % YL * X + (x + dx) % X
+        part = KVT.at[:, :, :, c, :, lanes(col, ROWS)]
+        other = KVT.at[:, :, :, o, :, lanes(col, ROWS)]
+        flow.arrival(("c", dx, ep), other, r_c.at[col])
+        return ("m", 64, ("c", dx, ep), lambda: w.send(part, part, s_c.at[dx, ep], r_c.at[col], s, mate))
+    for dx in range(X):
+        for ep in range(YL):
+            if dx:
+                after = [("x", dx, e) for e in range(ep, 8, 2)]
+            else:
+                after = [("b", e) if e else "kr" for e in range(ep, 8, 2)]
+            flow.task(("cs", dx, ep), after=after, sends=[c_send(dx, ep)])
+            flow.task(("c", dx, ep), needs=[("c", dx, ep)])
+
+    def q_work():
+        q = QP[c] + QR[...]
+        q1, q2 = q[:64], q[64:]
+        co, si = COS[...], SIN[...]
+        qt = jnp.concatenate([q1 * co - q2 * si, q2 * co + q1 * si], axis=0)
+        QB[...] = jnp.transpose(qt).astype(BF16)
+    flow.arrival(("qr",), QR, r_q)
+    flow.task("q", needs=[("qr",)], work=q_work, cost=0.3, rank=1)
+    flow.emit(recv)
+
+    pick = T["pick"]
     kt = KVT[0].reshape(HD, SEQ)
     vt = KVT[1].reshape(HD, SEQ)
     CH = 64
@@ -390,7 +535,7 @@
     for zz in zpeers:
         recv(QZ.at[zz], r_e3.at[zz])
         out = out + QZ[zz]
-    kvload.wait()
+    T["kvload"].wait()
     recv(DKV.at[z, o], r_d4.at[z, o])
     for zz in zpeers:
         recv(DKV.at[zz, 0], r_d4.at[zz, 0])
@@ -442,14 +587,14 @@
             VMEM((ROWS, FB), BF16),
             pltpu.SMEM((4,), jnp.int32),
             VMEM((1, NP), jnp.int32),
-            DMA((3,)), DMA((Z * YH,)), DMA((YH,)), DMA((2, 4, YH)),
+            DMA((76,)), DMA((2, 2, Z * YH)),
             DMA(()), DMA(()), DMA(()),
             DMA((Z - 1,)), DMA((Z,)), DMA((YH - 1,)), DMA((YH,)),
-            DMA(()), DMA(()), DMA((X - 1, YL)), DMA((X, YL)),
+            DMA(()), DMA(()), DMA((6,)), DMA((X * YL,)),
             DMA(()), DMA(()),
             DMA((YH * YL - 1,)), DMA((YH, YL)),
-            DMA((YH * YL, X - 1)), DMA((X, YH, YL)),
-            DMA((X, YL)), DMA((X, YL)),
+            DMA((24,)), DMA((X, YH, YL)),
+            DMA((X, YL)), DMA((X * YL,)),
             DMA(()), DMA(()), DMA(()), DMA((5,)),
             DMA(()), DMA(()),
             DMA((X, C)), DMA((X, C)),

time: 86.9 us -> 88.5 us (1.018)
  Pallas kernels: 83.3 us -> 84.9 us
    pallas_call x1, Pallas kernels: 83.3 us -> 84.9 us  [per_device(): pl.pallas_call(whole, out_shape=(jax.ShapeDtypeStruct((ROWS, HD), BF16),...]
where the time goes in v3:
time: 88.5 us; the launch traced here: 88.3 us
  Pallas kernels  84.9 us (96%)
  local copies, waits for them, and re-layouts  2.77 us (3%)
    pallas_call x1, Pallas kernels, per_device(): pl.pallas_call(whole, out_shape=(jax.ShapeDtypeStruct((ROWS, HD), BF16),...  84.9 us
    unnamed x2, local copies, waits for them, and re-layouts  2.77 us

profile of v3, /device:TPU:1, one launch (start us, length us, event | category | flops | bytes accessed | tf_op | source)
XLA Modules:
  0.0 88.3 jit_solution(4368616527522200895)
XLA Ops:
  0.6 84.9 %whole.1 = (bf16[256,128]{1,0:T(8,128)(2,1)}, f32[16,128]{1,0:T(8,128)}) custom-call(bf16[256,128]{1,0:T(8,128)(2,1)} %hid.1, bf16[128,8192]{1,0:T(8,128)(2,1)} %qw.1, bf16[8,2,2,2,32,128]{5,4,3,2,1,0:T(8,128)(2,1)} %bitcast.2, bf16[2048,128]{1,0:T(8,128)(2,1)} %kvflat.1, bf16[256,128]{1,0:T(8,128)(2,1)} %dhbm.1, s32[4]{0:T(128)} %dochbm.1, s32[1,128]{1,0:T(1,128)} %bitcast.3), custom_call_target="tpu_custom_call" | custom-call | tf_op jit(solution)/shard_map/whole/pallas_call | solution.py:551
  85.5 1.5 %copy.10 = bf16[256,128]{1,0:T(8,128)(2,1)} copy(bf16[256,128]{1,0:T(8,128)(2,1)} %get-tuple-element.4) | data formatting | bytes 131072
  87.0 1.3 %copy.11 = f32[16,128]{1,0:T(8,128)} copy(f32[16,128]{1,0:T(8,128)} %get-tuple-element.5) | data formatting | bytes 16384

commit v4 on v3

--- a/solution.py
+++ b/solution.py
@@ -16,6 +16,8 @@
 DMA = pltpu.SemaphoreType.DMA
 
 X, YL, YH, Z, C = 4, 2, 4, 8, 2
+ZROWS = 32
+KINDS = "YZ" if ZROWS else "Y"
 ROWS, HD, FB = 256, 128, 128
 
 
@@ -185,8 +187,9 @@
     hown.start()
     flow = Flow()
     used = [0]
-    ROW = {"Y": {"F": (0, 192), "A": (0, 96), "B": (96, 96)},
-           "Z": {"F": (192, 64), "A": (192, 32), "B": (224, 32)}}
+    ny, nz = ROWS - ZROWS, ZROWS
+    ROW = {"Y": {"F": (0, ny), "A": (0, ny // 2), "B": (ny // 2, ny // 2)},
+           "Z": {"F": (ny, nz), "A": (ny, nz // 2), "B": (ny + nz // 2, nz // 2)}}
 
     def hpiece(kind, dz, dy, h):
         r0, n = ROW[kind][h]
@@ -208,7 +211,7 @@
         return (way, n / 4, (kind, (dz - ez) % Z, (dy - ey) % YH, h), go)
 
     def hidden_tasks():
-        for kind in "YZ":
+        for kind in KINDS:
             for dz in range(Z):
                 for dy in range(YH):
                     two = dy == 2 and (kind == "Z" or dz == 0) or dz == 4 and (kind == "Y" or dy == 0)
@@ -236,7 +239,11 @@
                             sends.append(("z+", "A" if dz == 5 else "F"))
                         elif dz < 4:
                             sends.append(("z-", "B" if dz == 3 else "F"))
-                        sends += [("y+", "F"), ("y-", "F")]
+                        if dz == 0:
+                            sends += [("y+", "F"), ("y-", "F")]
+                        else:
+                            flow.task(("Zy", dz), after=[("Z", dz, 0), ("Y", 0, 1), ("Y", 0, 3)], rank=1,
+                                      sends=[hsend(kind, dz, dy, "F", way) for way in ("y+", "y-")])
                     elif dy == 3:
                         sends.append(("y+", "A"))
                     elif dy == 1:
@@ -364,7 +371,7 @@
     flow.task("wq0", sends=[("n", 8, ("wq",), lambda: None)], rank=-3)
     flow.task("wq", after=["wq0", ("Y", 0, 2)], work=wq_work, cost=0.3, rank=1)
     for dz in range(Z):
-        chunk_of = [(kind, dz, dy) for kind in "YZ" for dy in range(YH)]
+        chunk_of = [(kind, dz, dy) for kind in KINDS for dy in range(YH)]
         flow.task(("gkv", dz), after=chunk_of + ["wq", "kwf"], cost=0.15, rank=1,
                   work=functools.partial(lambda i: gain_kv((z + i) % Z), dz))
         flow.task(("gq", dz), after=chunk_of + ["wq"], cost=0.32, rank=2,
@@ -492,19 +499,18 @@
     recv(QG.at[o], r_g)
     both = jnp.concatenate([QG[0], QG[1]], axis=1)
 
-    def spread(zz, _):
+    for e in (4, 3, 5, 2, 6, 1, 7, 0):
+        zz = (z + e) % Z
         part = nn(both, W2[:, pl.ds(pl.multiple_of(zz * 512, 512), 512)])
         for yy in range(YH):
-            QF[yy, zz] = part[:, yy * 128:(yy + 1) * 128].astype(BF16)
-        QS[zz] = jnp.zeros((PL, HD), F32)
-        for yy in range(YH):
-            QS[zz] = QS[zz] + jnp.where(yy == yh, part[:, yy * 128:(yy + 1) * 128], 0.0)
-        return 0
-    lax.fori_loop(0, Z, spread, 0)
-
-    for e in range(1, YH):
-        yy = (yh + e) % YH
-        w.send(QF.at[yy], QY.at[yh], s_e2.at[e - 1], r_e2.at[yh], s, d.fid(z, yy, c))
+            piece = part[:, yy * 128:(yy + 1) * 128]
+            if e:
+                QF[zz, yy] = piece.astype(BF16)
+            else:
+                QS[yy] = piece
+        if e:
+            w.send(QF.at[zz], QY.at[z], s_e2.at[e - 1], r_e2.at[z], s, d.fid(zz, yh, c))
+
     recv(GX.at[x, o], r_d2.at[x, o])
     acc = GP[c, :, x] + GX[x, o]
     for xx in xpeers:
@@ -514,12 +520,6 @@
     G2[...] = acc
     for e, (yy, ll) in enumerate(ypeers):
         w.send(G2.at[ll], GY.at[yh, yl], s_d3.at[e], r_d3.at[yh, yl], ll * X + x, d.fid(z, yy, c))
-    for e in range(1, YH):
-        yy = (yh + e) % YH
-        recv(QY.at[yy], r_e2.at[yy])
-        QS[...] = QS[...] + QY[yy].astype(F32)
-    for e, zz in enumerate(zpeers):
-        w.send(QS.at[zz], QZ.at[z], s_e3.at[e], r_e3.at[z], s, d.fid(zz, yh, c))
     acc = G2[yl]
     for yy, ll in ypeers:
         recv(GY.at[yy, ll], r_d3.at[yy, ll])
@@ -531,17 +531,22 @@
     for e, zz in enumerate(zpeers):
         for i, cc in enumerate((c, o)):
             w.send(DK, DKV.at[z, c], s_d4.at[e, i], r_d4.at[z, c], s, d.fid(zz, yh, cc))
-    out = QS[z]
     for zz in zpeers:
-        recv(QZ.at[zz], r_e3.at[zz])
-        out = out + QZ[zz]
+        recv(QY.at[zz], r_e2.at[zz])
+        QS[...] = QS[...] + QY[zz].astype(F32)
+    for e, yy in enumerate(ysides):
+        w.send(QS.at[yy], QZ.at[yh], s_e3.at[e], r_e3.at[yh], s, d.fid(z, yy, c))
     T["kvload"].wait()
     recv(DKV.at[z, o], r_d4.at[z, o])
     for zz in zpeers:
         recv(DKV.at[zz, 0], r_d4.at[zz, 0])
         recv(DKV.at[zz, 1], r_d4.at[zz, 1])
     wide = jnp.concatenate([DKV[g, p] for g in range(Z) for p in range(2)], axis=1)
-    pg_out[...] = out + nn(wide, KVL[...])
+    out = QS[yh] + nn(wide, KVL[...])
+    for yy in ysides:
+        recv(QZ.at[yy], r_e3.at[yy])
+        out = out + QZ[yy]
+    pg_out[...] = out
     w.finish()
 
 
@@ -580,10 +585,10 @@
             VMEM((YH, YL, PL, HD), F32),
             VMEM((PL, HD), BF16),
             VMEM((Z, 2, PL, HD), BF16),
-            VMEM((YH, Z, PL, HD), BF16),
-            VMEM((YH, Z, PL, HD), BF16),
-            VMEM((Z, PL, HD), F32),
-            VMEM((Z, PL, HD), F32),
+            VMEM((Z, YH, PL, HD), BF16),
+            VMEM((Z, YH, PL, HD), BF16),
+            VMEM((YH, PL, HD), F32),
+            VMEM((YH, PL, HD), F32),
             VMEM((ROWS, FB), BF16),
             pltpu.SMEM((4,), jnp.int32),
             VMEM((1, NP), jnp.int32),
@@ -600,8 +605,8 @@
             DMA((X, C)), DMA((X, C)),
             DMA((YH * YL - 1,)), DMA((YH, YL)),
             DMA((Z, 2)), DMA((Z, 2)),
+            DMA((Z - 1,)), DMA((Z,)),
             DMA((YH - 1,)), DMA((YH,)),
-            DMA((Z - 1,)), DMA((Z,)),
         ],
         compiler_params=pltpu.CompilerParams(
             collective_id=0, has_side_effects=True, vmem_limit_bytes=67043328),

time: 88.5 us -> 86.7 us (0.980)
  Pallas kernels: 84.9 us -> 83.1 us
    pallas_call x1, Pallas kernels: 84.9 us -> 83.1 us  [per_device(): pl.pallas_call(whole, out_shape=(jax.ShapeDtypeStruct((ROWS, HD), BF16),...]
where the time goes in v4:
time: 86.7 us; the launch traced here: 86.5 us
  Pallas kernels  83.1 us (96%)
  local copies, waits for them, and re-layouts  2.77 us (3%)
    pallas_call x1, Pallas kernels, per_device(): pl.pallas_call(whole, out_shape=(jax.ShapeDtypeStruct((ROWS, HD), BF16),...  83.1 us
    unnamed x2, local copies, waits for them, and re-layouts  2.77 us

profile of v4, /device:TPU:1, one launch (start us, length us, event | category | flops | bytes accessed | tf_op | source)
XLA Modules:
  0.0 86.5 jit_solution(14754918404424627351)
XLA Ops:
  0.6 83.1 %whole.1 = (bf16[256,128]{1,0:T(8,128)(2,1)}, f32[16,128]{1,0:T(8,128)}) custom-call(bf16[256,128]{1,0:T(8,128)(2,1)} %hid.1, bf16[128,8192]{1,0:T(8,128)(2,1)} %qw.1, bf16[8,2,2,2,32,128]{5,4,3,2,1,0:T(8,128)(2,1)} %bitcast.2, bf16[2048,128]{1,0:T(8,128)(2,1)} %kvflat.1, bf16[256,128]{1,0:T(8,128)(2,1)} %dhbm.1, s32[4]{0:T(128)} %dochbm.1, s32[1,128]{1,0:T(1,128)} %bitcast.3), custom_call_target="tpu_custom_call" | custom-call | tf_op jit(solution)/shard_map/whole/pallas_call | solution.py:556
  83.7 1.5 %copy.10 = bf16[256,128]{1,0:T(8,128)(2,1)} copy(bf16[256,128]{1,0:T(8,128)(2,1)} %get-tuple-element.4) | data formatting | bytes 131072
  85.2 1.3 %copy.11 = f32[16,128]{1,0:T(8,128)} copy(f32[16,128]{1,0:T(8,128)} %get-tuple-element.5) | data formatting | bytes 16384

commit v5 on v4

--- a/solution.py
+++ b/solution.py
@@ -36,6 +36,12 @@
         self.c = self.f % C
         self.o = 1 - self.c
 
+    def hop(self, z, yh):
+        return (self.c + z + self.z + yh + self.yh) % 2
+
+    def far(self, z, yh):
+        return self.fid(z, yh, self.hop(z, yh))
+
     def fid(self, z, yh, c):
         return (z * YH + yh) * C + c
 
@@ -68,8 +74,8 @@
 
 
 class Flow:
-    RATE = {"z+": 45.0, "z-": 45.0, "y+": 22.0, "y-": 22.0, "x+": 45.0, "x-": 45.0, "m": 300.0, "n": 1e9}
-    LAG = {"z+": 1.7, "z-": 1.7, "y+": 2.5, "y-": 2.5, "x+": 1.7, "x-": 1.7, "m": 0.9, "n": 4.0}
+    RATE = {"z+": 45.0, "z-": 45.0, "y+": 22.0, "y-": 22.0, "x+": 45.0, "x-": 45.0, "x2": 22.0, "m": 300.0, "n": 1e9}
+    LAG = {"z+": 2.1, "z-": 2.1, "y+": 2.9, "y-": 2.9, "x+": 2.1, "x-": 2.1, "x2": 2.8, "m": 1.0, "n": 4.0}
 
     def __init__(self):
         self.tasks = {}
@@ -159,6 +165,8 @@
         y = (yh * YL + yl + e) % (YH * YL)
         ypeers.append((y // YL, y % YL))
         peers.append(((y % YL) * X + x, d.fid(z, y // YL, c)))
+    for e in (1, 3):
+        peers.append((s, d.fid(z, (yh + e) % YH, o)))
     xpeers = [(x + e) % X for e in range(1, X)]
     for xx in xpeers:
         peers.append((yl * X + xx, f))
@@ -180,26 +188,27 @@
     def eighth(g):
         return kvw.at[g, :, s // 4, :, pl.ds(pl.multiple_of((s % 4) * 8, 8), 8), :]
     for e, zz in enumerate(zpeers):
-        w.send(eighth(zz), KZ.at[z], s_kz.at[e], r_kz.at[z], s, d.fid(zz, yh, c))
+        w.send(eighth(zz), KZ.at[z], s_kz.at[e], r_kz.at[z], s, d.far(zz, yh))
     kzown = pltpu.make_async_copy(eighth(z), KZ.at[z], l_in.at[3])
     kzown.start()
     hown = pltpu.make_async_copy(hid, hblock(z, yh), l_in.at[4])
     hown.start()
     flow = Flow()
     used = [0]
-    ny, nz = ROWS - ZROWS, ZROWS
-    ROW = {"Y": {"F": (0, ny), "A": (0, ny // 2), "B": (ny // 2, ny // 2)},
-           "Z": {"F": (ny, nz), "A": (ny, nz // 2), "B": (ny + nz // 2, nz // 2)}}
+    ny = ROWS - ZROWS
+    ROW = {"Y": {"A": (0, ny // 2), "B": (ny // 2, ny // 2)}, "Z": {"A": (ny, ZROWS // 2), "B": (ny + ZROWS // 2, ZROWS // 2)}}
+    REACH = {"A": {"z+": 4, "z-": 3, "y+": 2, "y-": 1}, "B": {"z+": 3, "z-": 4, "y+": 1, "y-": 2}}
+    STEPS = {"z+": (1, 0), "z-": (-1, 0), "y+": (0, 1), "y-": (0, -1)}
 
     def hpiece(kind, dz, dy, h):
         r0, n = ROW[kind][h]
         return H.at[pl.ds(r0, n), lanes((z + dz) % Z * YH + (yh + dy) % YH)]
 
     def hsem(kind, dz, dy, h):
-        return r_h.at[0 if kind == "Y" else 1, 1 if h == "B" else 0, (z + dz) % Z * YH + (yh + dy) % YH]
+        return r_h.at["YZ".index(kind), "AB".index(h), (z + dz) % Z * YH + (yh + dy) % YH]
 
     def hsend(kind, dz, dy, h, way):
-        ez, ey = {"z+": (1, 0), "z-": (-1, 0), "y+": (0, 1), "y-": (0, -1)}[way]
+        ez, ey = STEPS[way]
         r0, n = ROW[kind][h]
         slot = s_h.at[used[0]]
         used[0] += 1
@@ -207,60 +216,58 @@
 
         def go():
             w.send(src, hpiece(kind, dz, dy, h), slot, hsem(kind, dz, dy, h),
-                   s, d.fid((z + ez) % Z, (yh + ey) % YH, c))
+                   s, d.fid((z + ez) % Z, (yh + ey) % YH, o))
         return (way, n / 4, (kind, (dz - ez) % Z, (dy - ey) % YH, h), go)
+
+    def onward(dist, size, h, up, down, first):
+        if dist == 0:
+            return [up, down] if first == up else [down, up]
+        out = []
+        back = size - dist
+        if back < REACH[h][up] and dist > size // 2:
+            out.append(up)
+        if dist < REACH[h][down] and dist < size // 2:
+            out.append(down)
+        return out
 
     def hidden_tasks():
         for kind in KINDS:
+            start = []
             for dz in range(Z):
                 for dy in range(YH):
-                    two = dy == 2 and (kind == "Z" or dz == 0) or dz == 4 and (kind == "Y" or dy == 0)
-                    needs = [(kind, dz, dy, h) for h in ("AB" if two else "F")] if dz or dy else []
-                    for key in needs:
-                        flow.arrival(key, hpiece(*key), hsem(*key))
-                    sends = []
-                    if kind == "Y":
-                        if dz == 0:
-                            if dy == 0:
-                                sends += [("y+", "F"), ("y-", "F")]
-                            if dy == 3:
-                                sends.append(("y+", "A"))
-                            if dy == 1:
-                                sends.append(("y-", "B"))
-                            sends += [("z+", "F"), ("z-", "F")]
-                        elif dz > 4:
-                            sends.append(("z+", "A" if dz == 5 else "F"))
-                        elif dz < 4:
-                            sends.append(("z-", "B" if dz == 3 else "F"))
-                    elif dy == 0:
-                        if dz == 0:
-                            sends += [("z+", "F"), ("z-", "F")]
-                        elif dz > 4:
-                            sends.append(("z+", "A" if dz == 5 else "F"))
-                        elif dz < 4:
-                            sends.append(("z-", "B" if dz == 3 else "F"))
-                        if dz == 0:
-                            sends += [("y+", "F"), ("y-", "F")]
+                    for h in "AB":
+                        name = (kind, dz, dy, h)
+                        needs = [name] if dz or dy else []
+                        if needs:
+                            flow.arrival(name, hpiece(*name), hsem(*name))
+                        alongz = onward(dz, Z, h, "z+", "z-", "z+" if h == "A" else "z-")
+                        alongy = onward(dy, YH, h, "y+", "y-", "y+" if h == "A" else "y-")
+                        if kind == "Y":
+                            ways = (alongy if dz == 0 else []) + alongz
+                            if dz == 0 and dy == 0:
+                                ways = [alongy[0], alongz[0], alongz[1], alongy[1]]
                         else:
-                            flow.task(("Zy", dz), after=[("Z", dz, 0), ("Y", 0, 1), ("Y", 0, 3)], rank=1,
-                                      sends=[hsend(kind, dz, dy, "F", way) for way in ("y+", "y-")])
-                    elif dy == 3:
-                        sends.append(("y+", "A"))
-                    elif dy == 1:
-                        sends.append(("y-", "B"))
-                    flow.task((kind, dz, dy), needs=needs,
-                              sends=[hsend(kind, dz, dy, h, way) for way, h in sends],
-                              rank=0 if dz or dy else (-2 if kind == "Z" else -1))
+                            ways = alongz if dy == 0 else alongy
+                        if kind == "Z" and dy == 0:
+                            after = [name] + ([("Y", 0, 1, "B"), ("Y", 0, 3, "A")] if dz else [])
+                            flow.task(("Zy", dz, h), after=after, rank=1,
+                                      sends=[hsend(kind, dz, dy, h, way) for way in alongy])
+                        if dz or dy:
+                            flow.task(name, needs=needs, sends=[hsend(kind, dz, dy, h, way) for way in ways])
+                        else:
+                            start += [(i, hsend(kind, dz, dy, h, way)) for i, way in enumerate(ways)]
+            start.sort(key=lambda pair: (pair[0] + 1) // 2)
+            flow.task((kind, 0, 0, "A"), sends=[send for _, send in start], rank=-1 if kind == "Z" else -2)
+            flow.task((kind, 0, 0, "B"), after=[(kind, 0, 0, "A")], rank=-2)
     hidden_tasks()
 
     T = {}
 
     def setup():
         def wload(k, _):
-            pltpu.make_async_copy(qw.at[:, pl.ds(pl.multiple_of(k * 256 + c * 128, 128), 128)],
-                                  W2.at[pl.ds(c * 128, 128), lanes(k)], l_w).start()
-            w.make(qw.at[:, pl.ds(pl.multiple_of(k * 256 + o * 128, 128), 128)],
-                   W2.at[pl.ds(c * 128, 128), lanes(k)], s_w, r_w, s, mate).start()
+            keep = d.hop(k // YH, k % YH)
+            pltpu.make_async_copy(qw.at[:, lanes(k * 2 + keep)], W2.at[pl.ds(c * 128, 128), lanes(k)], l_w).start()
+            w.make(qw.at[:, lanes(k * 2 + 1 - keep)], W2.at[pl.ds(c * 128, 128), lanes(k)], s_w, r_w, s, mate).start()
             return 0
         lax.fori_loop(0, Z * YH, wload, 0)
         kvload = pltpu.make_async_copy(kvflat, KVL, l_v)
@@ -293,7 +300,7 @@
     def back(u):
         return u * T["cos_p"] + pltpu.roll(u, 64, 1) * T["sin_p"]
 
-    flow.task("setup", after=[("Y", 0, 0)], work=setup, cost=1.0, rank=-1)
+    flow.task("setup", after=[("Y", 0, 0, "A"), ("Y", 0, 0, "B")], work=setup, cost=1.0, rank=-1)
 
     def gain(zz):
         cols = pl.ds(pl.multiple_of(zz * 512, 512), 512)
@@ -313,7 +320,7 @@
     ysides = [(yh + e) % YH for e in range(1, YH)]
 
     def ky_go(e, yy):
-        return lambda: w.send(KZ.at[:, yy // 2, yy % 2], KY.at[yh], s_ky.at[e], r_ky.at[yh], s, d.fid(z, yy, c))
+        return lambda: w.send(KZ.at[:, yy // 2, yy % 2], KY.at[yh], s_ky.at[e], r_ky.at[yh], s, d.far(z, yy))
 
     def kz_work():
         kzown.wait()
@@ -369,9 +376,9 @@
         QP[...] = jnp.zeros_like(QP)
         KP[...] = jnp.zeros_like(KP)
     flow.task("wq0", sends=[("n", 8, ("wq",), lambda: None)], rank=-3)
-    flow.task("wq", after=["wq0", ("Y", 0, 2)], work=wq_work, cost=0.3, rank=1)
+    flow.task("wq", after=["wq0", ("Y", 0, 2, "A")], work=wq_work, cost=0.3, rank=1)
     for dz in range(Z):
-        chunk_of = [(kind, dz, dy) for kind in KINDS for dy in range(YH)]
+        chunk_of = [(kind, dz, dy, h) for kind in KINDS for dy in range(YH) for h in "AB"]
         flow.task(("gkv", dz), after=chunk_of + ["wq", "kwf"], cost=0.15, rank=1,
                   work=functools.partial(lambda i: gain_kv((z + i) % Z), dz))
         flow.task(("gq", dz), after=chunk_of + ["wq"], cost=0.32, rank=2,
@@ -396,10 +403,11 @@
         KVT[yh // 2, :, yh % 2, c, :, lanes(s, ROWS)] = KB[...]
 
     yrel = [(yh, yl)] + ypeers
+    LATE = (3, 4)
     used.append(0)
 
     def x_send(dx, e, way):
-        ex = 1 if way == "x+" else -1
+        ex = {"x+": 1, "x-": -1, "x2": 2}[way]
         yy, ll = yrel[e]
         block = kblock(yy, ll, (x + dx) % X)
         src = KB if (dx, e) == (0, 0) else block
@@ -419,16 +427,17 @@
     for e in range(1, YH * YL):
         yy, ll = yrel[e]
         flow.arrival(("b", e), kblock(yy, ll, x), r_b.at[yy, ll])
-        flow.task(("b", e), needs=[("b", e)], sends=[x_send(0, e, "x+"), x_send(0, e, "x-")])
+        flow.task(("b", e), needs=[("b", e)], sends=([x_send(0, e, "x2")] if e in LATE else []) + [
+            x_send(0, e, "x+"), x_send(0, e, "x-")])
     for e in range(YH * YL):
         yy, ll = yrel[e]
         for dx in range(1, X):
             xx = (x + dx) % X
             flow.arrival(("x", dx, e), kblock(yy, ll, xx), r_x.at[xx, yy, ll])
             sends = []
-            if dx == 3 and e % 2 == 0:
+            if dx == 3 and e % 2 == 0 and e not in LATE:
                 sends = [x_send(dx, e, "x+")]
-            if dx == 1 and e % 2 == 1:
+            if dx == 1 and e % 2 == 1 and e not in LATE:
                 sends = [x_send(dx, e, "x-")]
             flow.task(("x", dx, e), needs=[("x", dx, e)], sends=sends)
 
@@ -509,7 +518,7 @@
             else:
                 QS[yy] = piece
         if e:
-            w.send(QF.at[zz], QY.at[z], s_e2.at[e - 1], r_e2.at[z], s, d.fid(zz, yh, c))
+            w.send(QF.at[zz], QY.at[z], s_e2.at[e - 1], r_e2.at[z], s, d.far(zz, yh))
 
     recv(GX.at[x, o], r_d2.at[x, o])
     acc = GP[c, :, x] + GX[x, o]
@@ -535,7 +544,7 @@
         recv(QY.at[zz], r_e2.at[zz])
         QS[...] = QS[...] + QY[zz].astype(F32)
     for e, yy in enumerate(ysides):
-        w.send(QS.at[yy], QZ.at[yh], s_e3.at[e], r_e3.at[yh], s, d.fid(z, yy, c))
+        w.send(QS.at[yy], QZ.at[yh], s_e3.at[e], r_e3.at[yh], s, d.far(z, yy))
     T["kvload"].wait()
     recv(DKV.at[z, o], r_d4.at[z, o])
     for zz in zpeers:
@@ -592,7 +601,7 @@
             VMEM((ROWS, FB), BF16),
             pltpu.SMEM((4,), jnp.int32),
             VMEM((1, NP), jnp.int32),
-            DMA((76,)), DMA((2, 2, Z * YH)),
+            DMA((124,)), DMA((2, 2, Z * YH)),
             DMA(()), DMA(()), DMA(()),
             DMA((Z - 1,)), DMA((Z,)), DMA((YH - 1,)), DMA((YH,)),
             DMA(()), DMA(()), DMA((6,)), DMA((X * YL,)),

time: 86.7 us -> 84.7 us (0.977)
  Pallas kernels: 83.1 us -> 81.1 us
    pallas_call x1, Pallas kernels: 83.1 us -> 81.1 us  [per_device(): pl.pallas_call(whole, out_shape=(jax.ShapeDtypeStruct((ROWS, HD), BF16),...]
where the time goes in v5:
time: 84.7 us; the launch traced here: 84.5 us
  Pallas kernels  81.1 us (96%)
  local copies, waits for them, and re-layouts  2.77 us (3%)
    pallas_call x1, Pallas kernels, per_device(): pl.pallas_call(whole, out_shape=(jax.ShapeDtypeStruct((ROWS, HD), BF16),...  81.1 us
    unnamed x2, local copies, waits for them, and re-layouts  2.77 us

profile of v5, /device:TPU:1, one launch (start us, length us, event | category | flops | bytes accessed | tf_op | source)
XLA Modules:
  0.0 84.5 jit_solution(981103649287739454)
XLA Ops:
  0.6 81.1 %whole.1 = (bf16[256,128]{1,0:T(8,128)(2,1)}, f32[16,128]{1,0:T(8,128)}) custom-call(bf16[256,128]{1,0:T(8,128)(2,1)} %hid.1, bf16[128,8192]{1,0:T(8,128)(2,1)} %qw.1, bf16[8,2,2,2,32,128]{5,4,3,2,1,0:T(8,128)(2,1)} %bitcast.2, bf16[2048,128]{1,0:T(8,128)(2,1)} %kvflat.1, bf16[256,128]{1,0:T(8,128)(2,1)} %dhbm.1, s32[4]{0:T(128)} %dochbm.1, s32[1,128]{1,0:T(1,128)} %bitcast.3), custom_call_target="tpu_custom_call" | custom-call | tf_op jit(solution)/shard_map/whole/pallas_call | solution.py:565
  81.7 1.5 %copy.10 = bf16[256,128]{1,0:T(8,128)(2,1)} copy(bf16[256,128]{1,0:T(8,128)(2,1)} %get-tuple-element.4) | data formatting | bytes 131072
  83.2 1.3 %copy.11 = f32[16,128]{1,0:T(8,128)} copy(f32[16,128]{1,0:T(8,128)} %get-tuple-element.5) | data formatting | bytes 16384

commit v6 on v5

--- a/solution.py
+++ b/solution.py
@@ -73,6 +73,9 @@
     return lax.dot_general(a, b, (((0,), (0,)), ((), ())), preferred_element_type=F32)
 
 
+LAZY = 1.5
+
+
 class Flow:
     RATE = {"z+": 45.0, "z-": 45.0, "y+": 22.0, "y-": 22.0, "x+": 45.0, "x-": 45.0, "x2": 22.0, "m": 300.0, "n": 1e9}
     LAG = {"z+": 2.1, "z-": 2.1, "y+": 2.9, "y-": 2.9, "x+": 2.1, "x-": 2.1, "x2": 2.8, "m": 1.0, "n": 4.0}
@@ -93,9 +96,11 @@
         while todo:
             best = None
             for i, name in enumerate(todo):
-                needs, after, _, _, _, rank = self.tasks[name]
+                needs, after, sends, work, _, rank = self.tasks[name]
                 if all(n in at for n in needs) and all(a in done for a in after):
                     ready = max([at[n] for n in needs] + [done[a] for a in after] + [0.0])
+                    if needs and not sends and work is None:
+                        ready += LAZY
                     cand = (max(ready, now), rank, i)
                     if best is None or cand < best:
                         best = cand
@@ -144,7 +149,7 @@
 
 def whole(hid, qw, kvw, kvflat, dhbm, dochbm, phbm, att_out, pg_out,
           H, W2, KZ, KY, KW, KWF, KP, KR, KB, QP, QR, KVT, COS, SIN, QB, PB, CM, KVL,
-          QG, GP, GX, G2, GY, DK, DKV, QF, QY, QS, QZ, dat, doc, prow,
+          QG, GP, GX, G2, GY, DK, DKV, QF, QY, QS, QZ, dat, doc, prow, BIAS,
           s_h, r_h, s_w, r_w, l_w, s_kz, r_kz, s_ky, r_ky, s_kl, r_kl, s_kx, r_kx,
           s_p, r_p, s_b, r_b, s_x, r_x, s_c, r_c, s_q, r_q, l_v, l_in,
           s_g, r_g, s_d2, r_d2, s_d3, r_d3, s_d4, r_d4, s_e2, r_e2, s_e3, r_e3):
@@ -159,22 +164,25 @@
     for load in loads:
         load.start()
     bar = pltpu.get_barrier_semaphore()
-    peers = [(s, mate)]
+    peers = []
     ypeers = []
     for e in range(1, YH * YL):
         y = (yh * YL + yl + e) % (YH * YL)
         ypeers.append((y // YL, y % YL))
+    xpeers = [(x + e) % X for e in range(1, X)]
+    zpeers = [(z + e) % Z for e in range(1, Z)]
+    for e in (4, 3, 5, 2, 6, 1, 7):
+        for cc in (c, o):
+            peers.append((s, d.fid((z + e) % Z, yh, cc)))
+    for e in (4, 3, 5, 2, 6, 1, 7):
+        y = (yh * YL + yl + e) % (YH * YL)
         peers.append(((y % YL) * X + x, d.fid(z, y // YL, c)))
+    for e in (2, 1, 3):
+        for ff in (f, mate):
+            peers.append((yl * X + (x + e) % X, ff))
     for e in (1, 3):
         peers.append((s, d.fid(z, (yh + e) % YH, o)))
-    xpeers = [(x + e) % X for e in range(1, X)]
-    for xx in xpeers:
-        peers.append((yl * X + xx, f))
-        peers.append((yl * X + xx, mate))
-    zpeers = [(z + e) % Z for e in range(1, Z)]
-    for zz in zpeers:
-        peers.append((s, d.fid(zz, yh, c)))
-        peers.append((s, d.fid(zz, yh, o)))
+    peers.append((s, mate))
     for ps, pf in peers:
         pl.semaphore_signal(bar, inc=1, device_id={"seq": ps, "fsdp": pf}, device_id_type=MESH)
     pl.semaphore_wait(bar, len(peers))
@@ -285,6 +293,13 @@
         for i in range(8):
             at = i * 256 + lax.broadcasted_iota(jnp.int32, (256, NP), 0)
             CM[pl.ds(i * 256, 256), :] = jnp.where(at == prompts, 1.0, 0.0).astype(BF16)
+        def mask(i, _):
+            t = s * ROWS + i * 32 + lax.broadcasted_iota(jnp.int32, (32, 1), 0)
+            j = lax.broadcasted_iota(jnp.int32, (32, SEQ), 1)
+            BIAS[pl.ds(pl.multiple_of(i * 32, 32), 32), :] = jnp.where(
+                (j >= openings(t, doc)) & (j <= t), 0.0, -jnp.inf)
+            return 0
+        lax.fori_loop(0, ROWS // 32, mask, 0)
         near = lax.broadcasted_iota(jnp.int32, (PL, NP), 1) == (
             s * PL + lax.broadcasted_iota(jnp.int32, (PL, NP), 0))
         own_p = jnp.sum(jnp.where(near, prompts.astype(F32), 0.0), axis=1, keepdims=True).astype(jnp.int32)
@@ -454,7 +469,7 @@
             else:
                 after = [("b", e) if e else "kr" for e in range(ep, 8, 2)]
             flow.task(("cs", dx, ep), after=after, sends=[c_send(dx, ep)])
-            flow.task(("c", dx, ep), needs=[("c", dx, ep)])
+            flow.task(("c", dx, ep), needs=[("c", dx, ep)], after=[("cs", i, j) for i in range(X) for j in range(YL)])
 
     def q_work():
         q = QP[c] + QR[...]
@@ -471,20 +486,13 @@
     vt = KVT[1].reshape(HD, SEQ)
     CH = 64
 
-    def chunk(i, _):
-        rows = pl.ds(pl.multiple_of(i * CH, CH), CH)
-        raw = nn(QB[rows, :], KVT[0].reshape(HD, SEQ)) * SCALE
-        t = s * ROWS + i * CH + lax.broadcasted_iota(jnp.int32, (CH, 1), 0)
-        start = openings(t, doc)
-        j = lax.broadcasted_iota(jnp.int32, (CH, SEQ), 1)
-        raw = jnp.where((j >= start) & (j <= t), raw, -jnp.inf)
-        top = jnp.max(raw, axis=1, keepdims=True)
-        e = jnp.exp(raw - top)
+    for i in range(ROWS // CH):
+        rows = pl.ds(i * CH, CH)
+        raw = nn(QB[rows, :], kt) * (SCALE * math.log2(math.e)) + BIAS[rows, :]
+        e = jnp.exp2(raw - jnp.max(raw, axis=1, keepdims=True))
         probs = (e * (1.0 / jnp.sum(e, axis=1, keepdims=True))).astype(BF16)
         PB[rows, :] = probs
-        att_out[rows, :] = nt(probs, KVT[1].reshape(HD, SEQ)).astype(BF16)
-        return 0
-    lax.fori_loop(0, ROWS // CH, chunk, 0)
+        att_out[rows, :] = nt(probs, vt).astype(BF16)
 
     att = att_out[...]
     da = dat[...]
@@ -601,6 +609,7 @@
             VMEM((ROWS, FB), BF16),
             pltpu.SMEM((4,), jnp.int32),
             VMEM((1, NP), jnp.int32),
+            VMEM((ROWS, SEQ), F32),
             DMA((124,)), DMA((2, 2, Z * YH)),
             DMA(()), DMA(()), DMA(()),
             DMA((Z - 1,)), DMA((Z,)), DMA((YH - 1,)), DMA((YH,)),
@@ -618,10 +627,11 @@
             DMA((YH - 1,)), DMA((YH,)),
         ],
         compiler_params=pltpu.CompilerParams(
-            collective_id=0, has_side_effects=True, vmem_limit_bytes=67043328),
+            collective_id=0, has_side_effects=True, vmem_limit_bytes=48 << 20),
         name="whole",
-    )(hidden, q_weight, kv_weight.reshape(Z, 2, 2, 2, 32, FB), kv_weight, d_attended,
-      doc_lengths, prompt_pos.reshape(1, NP))
+    )(*(pltpu.with_memory_space_constraint(a, pltpu.HBM) for a in (
+        hidden, q_weight, kv_weight.reshape(Z, 2, 2, 2, 32, FB), kv_weight, d_attended,
+        doc_lengths, prompt_pos.reshape(1, NP))))
 
 
 def solution(mesh):

time: 84.7 us -> 80.3 us (0.948)
  Pallas kernels: 81.1 us -> 78.3 us
  local copies, waits for them, and re-layouts: 2.77 us -> 1.23 us
    pallas_call x1, Pallas kernels: 81.1 us -> 78.3 us  [per_device(): pl.pallas_call(whole, out_shape=(jax.ShapeDtypeStruct((ROWS, HD), BF16),...]
    unnamed x2, local copies, waits for them, and re-layouts: 2.77 us -> 1.23 us
where the time goes in v6:
time: 80.3 us; the launch traced here: 80.2 us
  Pallas kernels  78.3 us (98%)
  local copies, waits for them, and re-layouts  1.23 us (2%)
    pallas_call x1, Pallas kernels, per_device(): pl.pallas_call(whole, out_shape=(jax.ShapeDtypeStruct((ROWS, HD), BF16),...  78.3 us

profile of v6, /device:TPU:1, one launch (start us, length us, event | category | flops | bytes accessed | tf_op | source)
XLA Modules:
  0.0 80.2 jit_solution(726370252301846060)
XLA Ops:
  0.6 78.3 %whole.1 = (bf16[256,128]{1,0:T(8,128)(2,1)S(1)}, f32[16,128]{1,0:T(8,128)S(1)}) custom-call(bf16[256,128]{1,0:T(8,128)(2,1)} %hid.1, bf16[128,8192]{1,0:T(8,128)(2,1)} %qw.1, bf16[8,2,2,2,32,128]{5,4,3,2,1,0:T(8,128)(2,1)} %bitcast.2, bf16[2048,128]{1,0:T(8,128)(2,1)} %kvflat.1, bf16[256,128]{1,0:T(8,128)(2,1)} %dhbm.1, s32[4]{0:T(128)} %dochbm.1, ...), custom_call_target="tpu_custom_call" | custom-call | tf_op jit(solution)/shard_map/whole/pallas_call | solution.py:573
  79.0 0.6 copy.10
  79.6 0.6 copy.11

commit v7 on v6

--- a/solution.py
+++ b/solution.py
@@ -113,7 +113,8 @@
                 start = max(free.get(link, 0.0), now)
                 free[link] = start + size / self.RATE[link]
                 if key is not None:
-                    at[key] = max(at.get(key, 0.0), free[link] + self.LAG[link])
+                    lag = self.LAG[link] if key[0] != "b" else 1.5 + 0.8 * min(key[1], 8 - key[1])
+                    at[key] = max(at.get(key, 0.0), free[link] + lag)
             out.append(name)
         self.model = done
         return out
@@ -177,6 +178,8 @@
     for e in (4, 3, 5, 2, 6, 1, 7):
         y = (yh * YL + yl + e) % (YH * YL)
         peers.append(((y % YL) * X + x, d.fid(z, y // YL, c)))
+        if e % 2:
+            peers.append(((y % YL) * X + x, d.fid(z, y // YL, o)))
     for e in (2, 1, 3):
         for ff in (f, mate):
             peers.append((yl * X + (x + e) % X, ff))
@@ -403,8 +406,9 @@
     flow.task("qx", after=[("gq", dz) for dz in range(Z)], rank=1,
               sends=[("m", 128, ("qr",), lambda: w.send(QP.at[o], QR, s_q, r_q, s, mate))])
 
-    def kblock(yy, ll, xx):
-        return KVT.at[yy // 2, :, yy % 2, c, :, lanes(ll * X + xx, ROWS)]
+    def kblock(e, dx):
+        yy, ll = yrel[e]
+        return KVT.at[yy // 2, :, yy % 2, (c + e + dx) % 2, :, lanes(ll * X + (x + dx) % X, ROWS)]
 
     def kr_work():
         total = KP[c] + KR[...]
@@ -418,37 +422,38 @@
         KVT[yh // 2, :, yh % 2, c, :, lanes(s, ROWS)] = KB[...]
 
     yrel = [(yh, yl)] + ypeers
-    LATE = (3, 4)
+    LATE = (4,)
     used.append(0)
 
     def x_send(dx, e, way):
         ex = {"x+": 1, "x-": -1, "x2": 2}[way]
         yy, ll = yrel[e]
-        block = kblock(yy, ll, (x + dx) % X)
+        block = kblock(e, dx)
         src = KB if (dx, e) == (0, 0) else block
         slot = s_x.at[used[2]]
         used[2] += 1
         return (way, 16, ("x", (dx - ex) % X, e), lambda: w.send(
-            src, block, slot, r_x.at[(x + dx) % X, yy, ll], yl * X + (x + ex) % X, f))
+            src, block, slot, r_x.at[(x + dx) % X, yy, ll], yl * X + (x + ex) % X,
+            f if ex == 2 else mate))
 
     def b_send(e):
         yy, ll = ypeers[e]
         return ("y+" if e < 4 else "y-", 16 * min(e + 1, 7 - e) / 4, ("b", 7 - e), lambda: w.send(
-            KB, kblock(yh, yl, x), s_b.at[e], r_b.at[yh, yl], ll * X + x, d.fid(z, yy, c)))
+            KB, kblock(0, 0), s_b.at[e], r_b.at[yh, yl], ll * X + x, d.fid(z, yy, (c + e + 1) % 2)))
 
     flow.arrival(("kr",), KR, r_p)
     flow.task("kr", needs=[("kr",)], work=kr_work, cost=0.2,
-              sends=[b_send(e) for e in (3, 2, 4, 1, 5, 0, 6)] + [x_send(0, 0, "x+"), x_send(0, 0, "x-")])
+              sends=[b_send(e) for e in (0, 6, 1, 5, 2, 4, 3)] + [x_send(0, 0, "x+"), x_send(0, 0, "x-")])
     for e in range(1, YH * YL):
         yy, ll = yrel[e]
-        flow.arrival(("b", e), kblock(yy, ll, x), r_b.at[yy, ll])
+        flow.arrival(("b", e), kblock(e, 0), r_b.at[yy, ll])
         flow.task(("b", e), needs=[("b", e)], sends=([x_send(0, e, "x2")] if e in LATE else []) + [
             x_send(0, e, "x+"), x_send(0, e, "x-")])
     for e in range(YH * YL):
         yy, ll = yrel[e]
         for dx in range(1, X):
             xx = (x + dx) % X
-            flow.arrival(("x", dx, e), kblock(yy, ll, xx), r_x.at[xx, yy, ll])
+            flow.arrival(("x", dx, e), kblock(e, dx), r_x.at[xx, yy, ll])
             sends = []
             if dx == 3 and e % 2 == 0 and e not in LATE:
                 sends = [x_send(dx, e, "x+")]
@@ -458,8 +463,8 @@
 
     def c_send(dx, ep):
         col = (yl + ep) % YL * X + (x + dx) % X
-        part = KVT.at[:, :, :, c, :, lanes(col, ROWS)]
-        other = KVT.at[:, :, :, o, :, lanes(col, ROWS)]
+        part = KVT.at[:, :, :, (c + ep + dx) % 2, :, lanes(col, ROWS)]
+        other = KVT.at[:, :, :, (o + ep + dx) % 2, :, lanes(col, ROWS)]
         flow.arrival(("c", dx, ep), other, r_c.at[col])
         return ("m", 64, ("c", dx, ep), lambda: w.send(part, part, s_c.at[dx, ep], r_c.at[col], s, mate))
     for dx in range(X):
@@ -496,6 +501,12 @@
 
     att = att_out[...]
     da = dat[...]
+    row_up = nn(pick, da)
+    row_dot = jnp.sum(row_up * nn(pick, att), axis=1, keepdims=True)
+    row_dp = nn(row_up.astype(BF16), vt)
+    row_ds = (nn(pick, PB[...]) * (row_dp - row_dot)).astype(BF16)
+    QG[c] = back(nt(row_ds, kt) * SCALE).astype(BF16)
+    w.send(QG.at[c], QG.at[c], s_g, r_g, s, mate)
     rowdot = jnp.sum(da.astype(F32) * att.astype(F32), axis=1, keepdims=True)
     colp = nn(PB[...], CM[...])
     cv = nn(vt, CM[...]).astype(BF16)
@@ -507,12 +518,7 @@
         for i, (pp, ff) in enumerate(((c, f), (o, mate))):
             if e or i:
                 w.send(GP.at[pp, :, xx], GX.at[x, c], s_d2.at[e, i], r_d2.at[x, c], yl * X + xx, ff)
-    row_up = nn(pick, da)
-    row_dot = jnp.sum(row_up * nn(pick, att), axis=1, keepdims=True)
-    row_dp = nn(row_up.astype(BF16), vt)
-    row_ds = (nn(pick, PB[...]) * (row_dp - row_dot)).astype(BF16)
-    QG[c] = back(nt(row_ds, kt) * SCALE).astype(BF16)
-    w.send(QG.at[c], QG.at[c], s_g, r_g, s, mate)
+
     recv(QG.at[o], r_g)
     both = jnp.concatenate([QG[0], QG[1]], axis=1)
 
@@ -535,7 +541,8 @@
             recv(GX.at[xx, cc], r_d2.at[xx, cc])
             acc = acc + GX[xx, cc]
     G2[...] = acc
-    for e, (yy, ll) in enumerate(ypeers):
+    for e in (3, 2, 4, 1, 5, 0, 6):
+        yy, ll = ypeers[e]
         w.send(G2.at[ll], GY.at[yh, yl], s_d3.at[e], r_d3.at[yh, yl], ll * X + x, d.fid(z, yy, c))
     acc = G2[yl]
     for yy, ll in ypeers:
@@ -544,10 +551,11 @@
     dkv = jnp.where(c == 0, back(acc * SCALE), acc).astype(BF16)
     DK[...] = dkv
     DKV[z, c] = dkv
-    w.send(DK, DKV.at[z, c], s_d4.at[Z - 1, 0], r_d4.at[z, c], s, mate)
-    for e, zz in enumerate(zpeers):
+    for e in (3, 2, 4, 1, 5, 0, 6):
+        zz = zpeers[e]
         for i, cc in enumerate((c, o)):
             w.send(DK, DKV.at[z, c], s_d4.at[e, i], r_d4.at[z, c], s, d.fid(zz, yh, cc))
+    w.send(DK, DKV.at[z, c], s_d4.at[Z - 1, 0], r_d4.at[z, c], s, mate)
     for zz in zpeers:
         recv(QY.at[zz], r_e2.at[zz])
         QS[...] = QS[...] + QY[zz].astype(F32)

time: 80.3 us -> 80.1 us (level)
  no operation moved by 1% of the time
where the time goes in v7:
time: 80.1 us; the launch traced here: 79.9 us
  Pallas kernels  78.1 us (98%)
  local copies, waits for them, and re-layouts  1.23 us (2%)
    pallas_call x1, Pallas kernels, per_device(): pl.pallas_call(whole, out_shape=(jax.ShapeDtypeStruct((ROWS, HD), BF16),...  78.1 us

profile of v7, /device:TPU:1, one launch (start us, length us, event | category | flops | bytes accessed | tf_op | source)
XLA Modules:
  0.0 79.9 jit_solution(14425988042259501349)
XLA Ops:
  0.6 78.1 %whole.1 = (bf16[256,128]{1,0:T(8,128)(2,1)S(1)}, f32[16,128]{1,0:T(8,128)S(1)}) custom-call(bf16[256,128]{1,0:T(8,128)(2,1)} %hid.1, bf16[128,8192]{1,0:T(8,128)(2,1)} %qw.1, bf16[8,2,2,2,32,128]{5,4,3,2,1,0:T(8,128)(2,1)} %bitcast.2, bf16[2048,128]{1,0:T(8,128)(2,1)} %kvflat.1, bf16[256,128]{1,0:T(8,128)(2,1)} %dhbm.1, s32[4]{0:T(128)} %dochbm.1, ...), custom_call_target="tpu_custom_call" | custom-call | tf_op jit(solution)/shard_map/whole/pallas_call | solution.py:581
  78.7 0.6 copy.10
  79.3 0.6 copy.11

commit v8 on v7

--- a/solution.py
+++ b/solution.py
@@ -150,7 +150,7 @@
 
 def whole(hid, qw, kvw, kvflat, dhbm, dochbm, phbm, att_out, pg_out,
           H, W2, KZ, KY, KW, KWF, KP, KR, KB, QP, QR, KVT, COS, SIN, QB, PB, CM, KVL,
-          QG, GP, GX, G2, GY, DK, DKV, QF, QY, QS, QZ, dat, doc, prow, BIAS,
+          QG, GP, GB, GX, G2, GY, DK, DKV, QF, QY, QS, QZ, dat, doc, prow, BIAS,
           s_h, r_h, s_w, r_w, l_w, s_kz, r_kz, s_ky, r_ky, s_kl, r_kl, s_kx, r_kx,
           s_p, r_p, s_b, r_b, s_x, r_x, s_c, r_c, s_q, r_q, l_v, l_in,
           s_g, r_g, s_d2, r_d2, s_d3, r_d3, s_d4, r_d4, s_e2, r_e2, s_e3, r_e3):
@@ -501,23 +501,26 @@
 
     att = att_out[...]
     da = dat[...]
+    rowdot = jnp.sum(da.astype(F32) * att.astype(F32), axis=1, keepdims=True)
+    gathered = nn(jnp.concatenate([PB[...], vt], axis=0), CM[...])
+    colp, cv = gathered[:ROWS], gathered[ROWS:].astype(BF16)
+    cds = (colp * (nn(da, cv) - rowdot)).astype(BF16)
+    kg = tn(cds, QB[...]).reshape(YL, X, PL, HD)
+    vg = tn(colp.astype(BF16), da).reshape(YL, X, PL, HD)
+    GB[0] = kg.astype(BF16)
+    GB[1] = vg.astype(BF16)
+    GP[...] = jnp.where(c == 0, kg, vg)
+    for e in (2, 1, 3, 0):
+        xx = (x + e) % X
+        for i, (pp, ff) in enumerate(((c, f), (o, mate))):
+            if e or i:
+                w.send(GB.at[pp, :, xx], GX.at[x, c], s_d2.at[e, i], r_d2.at[x, c], yl * X + xx, ff)
     row_up = nn(pick, da)
     row_dot = jnp.sum(row_up * nn(pick, att), axis=1, keepdims=True)
     row_dp = nn(row_up.astype(BF16), vt)
     row_ds = (nn(pick, PB[...]) * (row_dp - row_dot)).astype(BF16)
     QG[c] = back(nt(row_ds, kt) * SCALE).astype(BF16)
     w.send(QG.at[c], QG.at[c], s_g, r_g, s, mate)
-    rowdot = jnp.sum(da.astype(F32) * att.astype(F32), axis=1, keepdims=True)
-    colp = nn(PB[...], CM[...])
-    cv = nn(vt, CM[...]).astype(BF16)
-    cds = (colp * (nn(da, cv) - rowdot)).astype(BF16)
-    GP[0] = tn(cds, QB[...]).reshape(YL, X, PL, HD)
-    GP[1] = tn(colp.astype(BF16), da).reshape(YL, X, PL, HD)
-    for e in range(X):
-        xx = (x + e) % X
-        for i, (pp, ff) in enumerate(((c, f), (o, mate))):
-            if e or i:
-                w.send(GP.at[pp, :, xx], GX.at[x, c], s_d2.at[e, i], r_d2.at[x, c], yl * X + xx, ff)
 
     recv(QG.at[o], r_g)
     both = jnp.concatenate([QG[0], QG[1]], axis=1)
@@ -535,11 +538,11 @@
             w.send(QF.at[zz], QY.at[z], s_e2.at[e - 1], r_e2.at[z], s, d.far(zz, yh))
 
     recv(GX.at[x, o], r_d2.at[x, o])
-    acc = GP[c, :, x] + GX[x, o]
+    acc = GP[:, x] + GX[x, o].astype(F32)
     for xx in xpeers:
         for cc in range(C):
             recv(GX.at[xx, cc], r_d2.at[xx, cc])
-            acc = acc + GX[xx, cc]
+            acc = acc + GX[xx, cc].astype(F32)
     G2[...] = acc
     for e in (3, 2, 4, 1, 5, 0, 6):
         yy, ll = ypeers[e]
@@ -604,8 +607,9 @@
             VMEM((SEQ, NP), BF16),
             VMEM((SEQ, FB), BF16),
             VMEM((2, PL, HD), BF16),
-            VMEM((2, YL, X, PL, HD), F32),
-            VMEM((X, C, YL, PL, HD), F32),
+            VMEM((YL, X, PL, HD), F32),
+            VMEM((2, YL, X, PL, HD), BF16),
+            VMEM((X, C, YL, PL, HD), BF16),
             VMEM((YL, PL, HD), F32),
             VMEM((YH, YL, PL, HD), F32),
             VMEM((PL, HD), BF16),

time: 80.1 us -> 79.1 us (0.988)
  Pallas kernels: 78.1 us -> 77.1 us
    pallas_call x1, Pallas kernels: 78.1 us -> 77.1 us  [per_device(): pl.pallas_call(whole, out_shape=(jax.ShapeDtypeStruct((ROWS, HD), BF16),...]
where the time goes in v8:
time: 79.1 us; the launch traced here: 79 us
  Pallas kernels  77.1 us (97%)
  local copies, waits for them, and re-layouts  1.23 us (2%)
    pallas_call x1, Pallas kernels, per_device(): pl.pallas_call(whole, out_shape=(jax.ShapeDtypeStruct((ROWS, HD), BF16),...  77.1 us

profile of v8, /device:TPU:1, one launch (start us, length us, event | category | flops | bytes accessed | tf_op | source)
XLA Modules:
  0.0 79.0 jit_solution(131813202219963661)
XLA Ops:
  0.6 77.1 %whole.1 = (bf16[256,128]{1,0:T(8,128)(2,1)S(1)}, f32[16,128]{1,0:T(8,128)S(1)}) custom-call(bf16[256,128]{1,0:T(8,128)(2,1)} %hid.1, bf16[128,8192]{1,0:T(8,128)(2,1)} %qw.1, bf16[8,2,2,2,32,128]{5,4,3,2,1,0:T(8,128)(2,1)} %bitcast.2, bf16[2048,128]{1,0:T(8,128)(2,1)} %kvflat.1, bf16[256,128]{1,0:T(8,128)(2,1)} %dhbm.1, s32[4]{0:T(128)} %dochbm.1, ...), custom_call_target="tpu_custom_call" | custom-call | tf_op jit(solution)/shard_map/whole/pallas_call | solution.py:584
  77.7 0.6 copy.10
  78.4 0.6 copy.11

commit v9 on v8

--- a/solution.py
+++ b/solution.py
@@ -502,8 +502,8 @@
     att = att_out[...]
     da = dat[...]
     rowdot = jnp.sum(da.astype(F32) * att.astype(F32), axis=1, keepdims=True)
-    gathered = nn(jnp.concatenate([PB[...], vt], axis=0), CM[...])
-    colp, cv = gathered[:ROWS], gathered[ROWS:].astype(BF16)
+    colp = nn(PB[...], CM[...])
+    cv = nn(vt, CM[...]).astype(BF16)
     cds = (colp * (nn(da, cv) - rowdot)).astype(BF16)
     kg = tn(cds, QB[...]).reshape(YL, X, PL, HD)
     vg = tn(colp.astype(BF16), da).reshape(YL, X, PL, HD)

time: 79.1 us -> 78.5 us (level)
  no operation moved by 1% of the time
where the time goes in v9:
time: 78.5 us; the launch traced here: 78.4 us
  Pallas kernels  76.5 us (97%)
  local copies, waits for them, and re-layouts  1.23 us (2%)
    pallas_call x1, Pallas kernels, per_device(): pl.pallas_call(whole, out_shape=(jax.ShapeDtypeStruct((ROWS, HD), BF16),...  76.5 us

profile of v9, /device:TPU:1, one launch (start us, length us, event | category | flops | bytes accessed | tf_op | source)
XLA Modules:
  0.0 78.4 jit_solution(16369650852967092250)
XLA Ops:
  0.6 76.5 %whole.1 = (bf16[256,128]{1,0:T(8,128)(2,1)S(1)}, f32[16,128]{1,0:T(8,128)S(1)}) custom-call(bf16[256,128]{1,0:T(8,128)(2,1)} %hid.1, bf16[128,8192]{1,0:T(8,128)(2,1)} %qw.1, bf16[8,2,2,2,32,128]{5,4,3,2,1,0:T(8,128)(2,1)} %bitcast.2, bf16[2048,128]{1,0:T(8,128)(2,1)} %kvflat.1, bf16[256,128]{1,0:T(8,128)(2,1)} %dhbm.1, s32[4]{0:T(128)} %dochbm.1, ...), custom_call_target="tpu_custom_call" | custom-call | tf_op jit(solution)/shard_map/whole/pallas_call | solution.py:584
  77.2 0.6 copy.10
  77.8 0.6 copy.11
